TPU v7x, 512 devices: a whole 4x8x8 slice. The times are simulated.
512 devices in a mesh: grp: 16 (over z_lo, y), dev: 32 (over x, z_hi, core).
Axes of the slice: x: 4, y: 8, z: 8 (z_hi: 4, z_lo: 2; z = z_hi * 2 + z_lo), core: 2. Of those that a mesh axis runs over, the one named last changes fastest.
Arguments:
- sketch: bfloat16 [1048576, 256], P(('grp', 'dev')), may hold values from -4 to 4
- marginal_std: float32 [1048576], P(('grp', 'dev')), may hold values from 0.1 to 10
- cov_tiles: bfloat16 [9, 256, 256], replicated, may hold values from 0 to 1
- tile_cols: int32 [4096, 9], P(('grp', 'dev')), may hold values from -1 to 4095, as said below
Outputs:
- basis: float32 [1048576, 256], P(('grp', 'dev'))
- factor: float32 [256, 256], replicated
Inputs may be any that keep to these rules, and one draw needn't show every extreme that they name: `tile_cols`: tile t holds one line of 256 cells. The lines lie in depth order, except that the order within each aligned block of 4 tiles is permuted. Entry e of the list of tile t is the tile that holds the line e - 4 lines from the line of t (entry 4 is t itself), or -1 where that line lies beyond the ends of the field.
All inputs are finite; a program needn't handle non-finite values.
Results may differ from a plain program's by a relative error of at most 0.0035.
Values may be sent and summed in bfloat16 or wider, within the bound.
A program may use at most 64 MiB of HBM per device.

v0:
```python
import jax
import jax.numpy as jnp
from jax import lax
from jax.sharding import PartitionSpec as P


def with_halo(block, sides, width):
    for axis, dim in sides:
        count = lax.axis_size(axis)
        forward = [(i, i + 1) for i in range(count - 1)]
        backward = [(target, source) for source, target in forward]
        low = lax.ppermute(
            lax.slice_in_dim(block, block.shape[dim] - width, None, axis=dim), axis, forward
        )
        high = lax.ppermute(lax.slice_in_dim(block, 0, width, axis=dim), axis, backward)
        block = jnp.concatenate([low, block, high], axis=dim)
    return block


def per_device(sketch, marginal_std, cov_tiles, tile_cols):
    row_count, column_count = sketch.shape
    tile_size = cov_tiles.shape[1]
    row_tiles = row_count // tile_size
    scaled = (sketch.astype(jnp.float32) * marginal_std[:, None]).astype(jnp.bfloat16)
    extended = with_halo(scaled, ((("grp", "dev"), 0),), row_tiles * tile_size)
    extended_tiles = extended.reshape(-1, tile_size, column_count)
    first_tile = lax.axis_index(("grp", "dev")) * row_tiles
    present = tile_cols >= 0
    local_cols = jnp.where(present, tile_cols - first_tile + row_tiles, 0)
    gathered = extended_tiles[local_cols.T]
    gathered = jnp.where(present.T[:, :, None, None], gathered, jnp.zeros((), jnp.bfloat16))
    products = jnp.einsum("eij,etjk->tik", cov_tiles, gathered, preferred_element_type=jnp.float32)
    latent_field = products.reshape(row_count, column_count) * marginal_std[:, None]
    total_rows = row_count * lax.axis_size("grp") * lax.axis_size("dev")
    gram_matrix = (
        jnp.dot(latent_field.T, latent_field, precision=lax.Precision.HIGHEST) / total_rows
    )
    gram_matrix = lax.psum(gram_matrix, ("grp", "dev"))
    lower_factor = jnp.linalg.cholesky(gram_matrix)
    basis = lax.linalg.triangular_solve(
        lower_factor, latent_field, left_side=False, lower=True, transpose_a=True
    )
    return (basis, lower_factor.T)


def solution(mesh):
    in_specs = (P(("grp", "dev"), None), P(("grp", "dev")), P(), P(("grp", "dev"), None))
    out_specs = (P(("grp", "dev"), None), P())
    return jax.shard_map(
        per_device, mesh=mesh, in_specs=in_specs, out_specs=out_specs, check_vma=False
    )
```

profile of v0, /device:TPU:1, one launch (start us, length us, event | category | flops | bytes accessed | tf_op | source)
XLA Modules:
  0.0 429.9 jit_solution(10741237708848555990)
XLA Ops:
  7.2 0.0 copy-start
  7.2 0.0 copy-start.7
  7.2 0.0 copy-start.8
  7.2 0.0 all-reduce.3.cloned.1.call-start
  7.2 1.6 multiply_convert_fusion
  8.9 7.2 %collective-permute-start = (bf16[2048,256]{1,0:T(8,128)(2,1)S(1)}, bf16[2048,256]{1,0:T(8,128)(2,1)S(1)}, u32[]{:S(2)}, u32[]{:S(2)}) collective-permute-start(bf16[2048,256]{1,0:T(8,128)(2,1)S(1)} %multiply_convert_fusion), channel_id=1, source_target_pairs={{0,1},{1,2},{2,3},{3,4},{4,5},{5,6},{6,7},{7,8},{8,9},{9,10},{10,1... | collective-permute-start | bytes 3145736 | tf_op jit(solution)/shard_map/ppermute | solution.py:12
  16.1 2.9 collective-permute-start.1
  19.0 0.0 copy-done.7
  19.1 0.0 copy-done.8
  19.1 0.1 copy.13
  19.2 0.1 reshape.62
  19.3 0.1 copy.12
  19.4 8.6 %collective-permute-done = bf16[2048,256]{1,0:T(8,128)(2,1)S(1)} collective-permute-done((bf16[2048,256]{1,0:T(8,128)(2,1)S(1)}, bf16[2048,256]{1,0:T(8,128)(2,1)S(1)}, u32[]{:S(2)}, u32[]{:S(2)}) %collective-permute-start) | collective-permute-done | bytes 1048608 | tf_op jit(solution)/shard_map/ppermute | solution.py:12
  28.0 20.8 %collective-permute-done.1 = bf16[2048,256]{1,0:T(8,128)(2,1)} collective-permute-done((bf16[2048,256]{1,0:T(8,128)(2,1)S(1)}, bf16[2048,256]{1,0:T(8,128)(2,1)}, u32[]{:S(2)}, u32[]{:S(2)}) %collective-permute-start.1) | collective-permute-done | bytes 1048608 | tf_op jit(solution)/shard_map/ppermute | solution.py:15
  48.8 2.8 pad_maximum_fusion
  51.6 7.8 %gather_fusion = bf16[72,256,256]{2,1,0:T(8,128)(2,1)} fusion(bf16[24,256,256]{2,1,0:T(8,128)(2,1)} %bitcast.60, s32[1024]{0:T(1024)S(1)} %pad_clamp_fusion), kind=kCustom, calls=%fused_computation | custom fusion | bytes 18874656 | tf_op jit(solution)/shard_map/gather | solution.py:30
  59.4 0.0 copy-done
  59.4 5.5 %fusion = f32[8,256,256,1]{1,2,0,3:T(8,128)S(1)} fusion(bf16[9,8,256,256]{3,2,1,0:T(8,128)(2,1)} %bitcast.61, pred[9,8]{1,0:T(8,128)(4,1)S(1)} %copy.12, bf16[9,256,256]{2,1,0:T(8,128)(2,1)S(1)} %copy-done), kind=kOutput, calls=%fused_computation.3 | convolution fusion | flops 2420637696 | bytes 12714056 | tf_op jit(solution)/shard_map/eij,etjk->tik/dot_general | solution.py:32
  64.9 0.0 copy-start.1
  64.9 1.3 copy-done.1
  66.2 4.8 %fusion.7 = f32[256,256]{0,1:T(8,128)} fusion(f32[8,256,256,1]{1,2,0,3:T(8,128)S(1)} %fusion, f32[8,256]{1,0:T(8,128)S(1)} %mul.33), kind=kOutput, calls=%fused_computation.16 | convolution fusion | flops 1611202560 | bytes 2367488 | tf_op jit(solution)/shard_map/dot_general | solution.py:36
  71.0 0.0 all-reduce.3.cloned.1.call-update
  71.1 1.9 bitcast_multiply_fusion
  73.0 268.5 %all-reduce.3.cloned.1.call-done = f32[256,256]{0,1:T(8,128)} async-done(((f32[256,256]{0,1:T(8,128)}), f32[256,256]{0,1:T(8,128)}) %all-reduce.3.cloned.1.call-update) | async-done | bytes 262160 | tf_op jit(solution)/shard_map/psum | solution.py:38
  341.5 1.1 copy.17
  342.6 1.0 fusion.11
  343.6 0.0 copy-start.4
  343.6 0.7 copy-done.4
  344.3 11.7 %cholesky.50 = f32[128,128]{1,0:T(8,128)S(1)} custom-call(f32[128,128]{1,0:T(8,128)S(1)} %cholesky.118), custom_call_target="Cholesky" | custom-call | tf_op jit(solution)/shard_map/jit(cholesky)/cholesky | solution.py:39
  356.0 0.0 copy-start.5
  356.1 0.6 copy-done.5
  356.7 10.4 %custom-call.14 = f32[1,128,128]{1,2,0:T(8,128)} custom-call(f32[1,128,128]{2,1,0:T(8,128)S(1)} %get-tuple-element.29), custom_call_target="InvertDiagBlocksLowerTriangular" | custom-call | tf_op jit(solution)/shard_map/jit(cholesky)/cholesky | solution.py:39
  367.1 0.9 cholesky.113
  368.0 1.1 constant_dynamic-update-slice_fusion.1
  369.0 1.7 convolution_subtract_fusion.1
  370.8 13.4 %cholesky.105 = f32[128,128]{1,0:T(8,128)} custom-call(f32[128,128]{1,0:T(8,128)} %convolution_subtract_fusion.1), custom_call_target="Cholesky" | custom-call | tf_op jit(solution)/shard_map/jit(cholesky)/cholesky | solution.py:39
  384.2 0.9 select_reduce_fusion
  385.0 0.0 copy-start.2
  385.0 0.7 compare_reduce_fusion
  387.1 0.0 copy-done.2
  387.1 1.7 fusion.13
  388.8 0.1 triangular_solve.58
  388.9 5.3 %while.1 = (s32[]{:T(128)}, f32[256,256]{1,0:T(8,128)S(1)}, s32[2,2]{1,0:T(2,128)S(1)}, f32[2,128,128]{2,1,0:T(8,128)}, s32[]{:T(128)}) while((s32[]{:T(128)}, f32[256,256]{1,0:T(8,128)S(1)}, s32[2,2]{1,0:T(2,128)S(1)}, f32[2,128,128]{2,1,0:T(8,128)}, s32[]{:T(128)}) %tuple.30), condition=%wide.while_cond, body=%wide.while_body.sunk | while | flops 2 | bytes 132705 | solution.py:40
  388.9 0.6 fusion.27
  389.5 2.1 bitcast_dynamic-update-slice_fusion.2
  391.6 0.6 fusion.27
  392.2 2.0 bitcast_dynamic-update-slice_fusion.2
  394.2 21.1 %custom-call.15 = f32[2,128,128]{1,2,0:T(8,128)} custom-call(f32[2,128,128]{2,1,0:T(8,128)} %get-tuple-element.9), custom_call_target="InvertDiagBlocksLowerTriangular" | custom-call | tf_op jit(solution)/shard_map/triangular_solve | solution.py:40
  415.3 1.9 fusion.8
  417.2 0.0 copy-start.6
  417.3 1.8 convolution_subtract_fusion
  419.1 0.0 copy-done.6
  419.1 1.1 fusion.14
  420.2 0.1 pad_maximum_fusion.1
  420.3 0.0 copy-start.3
  420.4 1.8 copy.18
  422.2 0.0 copy-done.3
  422.2 0.8 copy.19
  (10 shorter events, 0.1 us)
Async XLA Ops:
  7.2 52.3 %copy-start = (bf16[9,256,256]{2,1,0:T(8,128)(2,1)S(1)}, bf16[9,256,256]{2,1,0:T(8,128)(2,1)}, u32[]{:S(2)}) copy-start(bf16[9,256,256]{2,1,0:T(8,128)(2,1)} %param.6) | copy-start | bytes 3538948
  7.2 11.8 %copy-start.7 = (f32[2048]{0:T(1024)S(1)}, f32[2048]{0:T(1024)}, u32[]{:S(2)}) copy-start(f32[2048]{0:T(1024)} %param.5) | copy-start | bytes 24580
  7.2 11.9 %copy-start.8 = (s32[8,9]{1,0:T(8,128)S(1)}, s32[8,9]{1,0:T(8,128)}, u32[]{:S(2)}) copy-start(s32[8,9]{1,0:T(8,128)} %param.7) | copy-start | bytes 868
  7.2 334.3 %all-reduce.3.cloned.1.call-start = ((), (), s32[]{:S(2)}) async-start(), calls=%async_computation | async-start | bytes 524288 | tf_op jit(solution)/shard_map/psum | solution.py:38
  8.9 19.1 %collective-permute-start = (bf16[2048,256]{1,0:T(8,128)(2,1)S(1)}, bf16[2048,256]{1,0:T(8,128)(2,1)S(1)}, u32[]{:S(2)}, u32[]{:S(2)}) collective-permute-start(bf16[2048,256]{1,0:T(8,128)(2,1)S(1)} %multiply_convert_fusion), channel_id=1, source_target_pairs={{0,1},{1,2},{2,3},{3,4},{4,5},{5,6},{6,7},{7,8},{8,9},{9,10},{10,1... | collective-permute-start | bytes 3145736 | tf_op jit(solution)/shard_map/ppermute | solution.py:12
  16.1 32.7 %collective-permute-start.1 = (bf16[2048,256]{1,0:T(8,128)(2,1)S(1)}, bf16[2048,256]{1,0:T(8,128)(2,1)}, u32[]{:S(2)}, u32[]{:S(2)}) collective-permute-start(bf16[2048,256]{1,0:T(8,128)(2,1)S(1)} %multiply_convert_fusion), channel_id=1, source_target_pairs={{1,0},{2,1},{3,2},{4,3},{5,4},{6,5},{7,6},{8,7},{9,8},{10,9},{11,1... | collective-permute-start | bytes 3145736 | tf_op jit(solution)/shard_map/ppermute | solution.py:15
  64.9 1.3 copy-start.1
  343.6 0.7 copy-start.4
  356.0 0.6 copy-start.5
  385.0 2.1 copy-start.2
  417.2 1.8 copy-start.6
  420.3 1.8 copy-start.3
Sparse Core Ops, SparseCore 0:
  71.2 270.2 all-reduce.2
where the time goes:
time: 431 us; the launch traced here: 430 us
  waiting for transfers between devices  298 us (69%)
  other arithmetic  67.5 us (16%)
  local copies, waits for them, and re-layouts  20.7 us (5%)
  matrix products  17.9 us (4%)
  between operations  15.6 us (4%)
  starting transfers between devices  10.1 us (2%)
    psum x1, waiting for transfers between devices, per_device(): gram_matrix = lax.psum(gram_matrix, ('grp', 'dev'))  269 us
    another operation x6, other arithmetic, per_device(): lower_factor = jnp.linalg.cholesky(gram_matrix)  37.2 us
    another operation x3, other arithmetic, per_device(): lax.linalg.triangular_solve(lower_factor, latent_field, left_side=False,...  21.2 us
    ppermute x1, waiting for transfers between devices, with_halo(): lax.ppermute(lax.slice_in_dim(block, 0, width, axis=dim), axis, backward)  20.8 us
    ppermute x1, waiting for transfers between devices, with_halo(): lax.ppermute(lax.slice_in_dim(block, block.shape[dim] - width, None, axis...  8.63 us
  transfers between devices with their start and end apart: 3, of which 3 were waited for; matrix products, arithmetic and copies ran while one was open for 1% of the time, Pallas kernels for 0%

commit v1 on v0

v1 whole, which is shorter than its diff:
```python
import functools

import jax
import jax.numpy as jnp
from jax import lax
from jax.experimental import pallas as pl
from jax.experimental.pallas import tpu as pltpu
from jax.sharding import PartitionSpec as P

MESH = pl.DeviceIdType.MESH
F32, BF16 = jnp.float32, jnp.bfloat16
REACH = 4
LINES = 8
LAGS = 9
PANEL = 32
PIVOT = 4

SIZES = dict(nx=4, ny=8, nzh=4, nzl=2)


def far_first(n):
    return sorted(range(1, n), key=lambda k: -min(k, n - k))


def front_kernel(
    sizes, scale, cols_ref, std_ref, sketch_hbm, cov_hbm, high_hbm, low_hbm, gram_ref,
    sketch_v, cov_v, own, below, above, std_sorted, std_cols, acc, high_v, low_v, gacc,
    packed, from_core, part_y, got_y, sum_y, got_z, sum_z, got_x, fin,
    load_sem, store_sem, halo_send, halo_recv, core_send, core_recv, y_send, y_recv,
    z_send, z_recv, x_send, x_recv, g_send, g_recv, f_send, f_recv,
):
    nx, ny, nzh, nzl = sizes["nx"], sizes["ny"], sizes["nzh"], sizes["nzl"]
    nz = nzh * nzl
    grp, dev = lax.axis_index("grp"), lax.axis_index("dev")
    per_grp = nx * nzh * 2
    total = per_grp * ny * nzl
    me = grp * per_grp + dev
    y, z_lo = lax.rem(grp, ny), lax.div(grp, ny)
    core = lax.rem(dev, 2)
    z_hi, x = lax.rem(lax.div(dev, 2), nzh), lax.div(dev, 2 * nzh)
    z = z_hi * nzl + z_lo

    def place(x_, y_, z_, core_):
        return (lax.rem(z_, nzl) * ny + y_, (x_ * nzh + lax.div(z_, nzl)) * 2 + core_)

    def linear(i):
        return (lax.div(i, per_grp), lax.rem(i, per_grp))

    mate = place(x, y, z, 1 - core)
    outer = jnp.where(core == 0, me - 1, me + 1)
    has_outer = (outer >= 0) & (outer < total)
    has_low, has_high = me > 0, me < total - 1

    load_sketch = pltpu.make_async_copy(sketch_hbm, sketch_v, load_sem.at[0])
    load_cov = pltpu.make_async_copy(cov_hbm, cov_v, load_sem.at[1])
    load_sketch.start()
    load_cov.start()

    barrier = pltpu.get_barrier_semaphore()

    def greet(device):
        pl.semaphore_signal(barrier, inc=1, device_id=device, device_id_type=MESH)

    y_peers = [(k, place(x, lax.rem(y + k, ny), z, core)) for k in far_first(ny)]
    z_peers = [(k, place(x, y, lax.rem(z + k, nz), core)) for k in far_first(nz)]
    x_peers = [(k, place(lax.rem(x + k, nx), y, z, core)) for k in far_first(nx)]
    for _, peer in z_peers + y_peers + x_peers:
        greet(peer)
    greet(mate)

    @pl.when(has_outer)
    def _():
        greet(linear(outer))

    tile_of_line = []
    for block in range(LINES // REACH):
        head = block * REACH
        start = cols_ref[head, REACH]
        offset = jnp.int32(0)
        for e in range(REACH):
            offset += jnp.where(cols_ref[head, e] >= start, 1, 0)
        for j in range(REACH):
            tile = cols_ref[head, REACH - offset + j] - start
            tile_of_line.append(jnp.clip(tile, 0, REACH - 1) + head)

    zero_lines = jnp.zeros((REACH,) + own.shape[1:], BF16)
    own[0:REACH] = zero_lines
    own[REACH + LINES :] = zero_lines

    @pl.when(jnp.logical_not(has_low))
    def _():
        below[...] = zero_lines

    @pl.when(jnp.logical_not(has_high))
    def _():
        above[...] = zero_lines

    for j in range(LINES):
        std_sorted[2 * j : 2 * j + 2, :] = std_ref[tile_of_line[j]]
    std_cols[...] = std_sorted[...].T

    def std_of(j):
        return jnp.concatenate([std_cols[:, 2 * j : 2 * j + 1], std_cols[:, 2 * j + 1 : 2 * j + 2]], axis=0)

    load_sketch.wait()
    for j in (0, 7, 1, 6, 2, 5, 3, 4):
        own[REACH + j] = (sketch_v[tile_of_line[j]].astype(F32) * std_of(j)).astype(BF16)
    gacc[...] = jnp.zeros_like(gacc)

    peers = len(y_peers) + len(z_peers) + len(x_peers) + 1
    pl.semaphore_wait(barrier, peers + jnp.where(has_outer, 1, 0))

    def to_low(q):
        return pltpu.make_async_remote_copy(
            src_ref=own.at[REACH + q], dst_ref=above.at[q], send_sem=halo_send.at[q],
            recv_sem=halo_recv.at[q], device_id=linear(me - 1), device_id_type=MESH,
        )

    def to_high(q):
        return pltpu.make_async_remote_copy(
            src_ref=own.at[REACH + LINES - 1 - q], dst_ref=below.at[q], send_sem=halo_send.at[REACH + q],
            recv_sem=halo_recv.at[REACH + q], device_id=linear(me + 1), device_id_type=MESH,
        )

    @pl.when(has_low)
    def _():
        for q in range(REACH):
            to_low(q).start()

    @pl.when(has_high)
    def _():
        for q in range(REACH):
            to_high(q).start()

    load_cov.wait()

    def own_line(j, carry):
        lags = jnp.concatenate([cov_v[e] for e in range(LAGS)], axis=1)
        lines = own[pl.ds(j, LAGS)].reshape(LAGS * own.shape[1], own.shape[2])
        acc[j] = jnp.dot(lags, lines, preferred_element_type=F32)
        return carry

    lax.fori_loop(0, LINES, own_line, 0)

    def finish(j, product):
        latent = product * std_of(j)
        high = latent.astype(BF16)
        low = (latent - high.astype(F32)).astype(BF16)
        high_v[j] = high
        low_v[j] = low
        pair = jnp.concatenate([high, low], axis=1)
        gacc[...] += lax.dot_general(high, pair, (((0,), (0,)), ((), ())), preferred_element_type=F32)
        pltpu.make_async_copy(high_v.at[j], high_hbm.at[j], store_sem.at[j]).start()
        pltpu.make_async_copy(low_v.at[j], low_hbm.at[j], store_sem.at[LINES + j]).start()

    for q in range(REACH):
        @pl.when(has_low)
        def _():
            to_high(q).wait_recv()

        for j in range(REACH - q):
            e = (-1 - q) - j + REACH
            product = acc[j] + jnp.dot(cov_v[e], below[q], preferred_element_type=F32)
            if j == REACH - 1 - q:
                finish(j, product)
            else:
                acc[j] = product

        @pl.when(has_high)
        def _():
            to_low(q).wait_recv()

        for j in range(REACH + q, LINES):
            e = (LINES + q) - j + REACH
            product = acc[j] + jnp.dot(cov_v[e], above[q], preferred_element_type=F32)
            if j == REACH + q:
                finish(j, product)
            else:
                acc[j] = product

    half = gacc.shape[0] // 2
    for n, (r, c) in enumerate(((0, 0), (0, half), (half, half))):
        hh = gacc[r : r + half, c : c + half]
        hl = gacc[r : r + half, 2 * half + c : 3 * half + c]
        lh = gacc[c : c + half, 2 * half + r : 3 * half + r].T
        packed[16 * n : 16 * n + 16] = ((hh + (hl + lh)) * scale).reshape(16, 8, 128)

    count = packed.shape[0] // 2
    chunk = count // ny
    swap = pltpu.make_async_remote_copy(
        src_ref=packed.at[pl.ds((1 - core) * count, count)], dst_ref=from_core, send_sem=core_send.at[0],
        recv_sem=core_recv.at[0], device_id=mate, device_id_type=MESH,
    )
    swap.start()
    swap.wait()
    part_y[...] = packed[pl.ds(core * count, count)] + from_core[...]

    copies = []
    for k, peer in y_peers:
        copies.append(pltpu.make_async_remote_copy(
            src_ref=part_y.at[pl.ds(lax.rem(y + k, ny) * chunk, chunk)], dst_ref=got_y.at[k],
            send_sem=y_send.at[k], recv_sem=y_recv.at[k], device_id=peer, device_id_type=MESH,
        ))
        copies[-1].start()
    value = part_y[pl.ds(y * chunk, chunk)]
    for k in range(1, ny):
        pltpu.make_async_copy(got_y.at[k], got_y.at[k], y_recv.at[k]).wait()
        value = value + got_y[k]

    def gather_sum(value, here, n, peers_, source, slots, send, recv):
        source[...] = value
        for k, peer in peers_:
            copies.append(pltpu.make_async_remote_copy(
                src_ref=source, dst_ref=slots.at[here], send_sem=send.at[k], recv_sem=recv.at[k],
                device_id=peer, device_id_type=MESH,
            ))
            copies[-1].start()
        slots[pl.ds(here, 1)] = value[None]
        for k in range(1, n):
            pltpu.make_async_copy(source, source, recv.at[k]).wait()
        out = slots[0]
        for i in range(1, n):
            out = out + slots[i]
        return out

    value = gather_sum(value, z, nz, z_peers, sum_y, got_z, z_send, z_recv)
    value = gather_sum(value, x, nx, x_peers, sum_z, got_x, x_send, x_recv)

    def chunk_of(y_):
        return fin.at[pl.ds(core * count + y_ * chunk, chunk)]

    def pass_on(k, y_):
        copies.append(pltpu.make_async_remote_copy(
            src_ref=chunk_of(y_), dst_ref=chunk_of(y_), send_sem=f_send.at[k], recv_sem=f_recv.at[k],
            device_id=mate, device_id_type=MESH,
        ))
        copies[-1].start()

    fin[pl.ds(core * count + y * chunk, chunk)] = value
    for k, peer in y_peers:
        copies.append(pltpu.make_async_remote_copy(
            src_ref=chunk_of(y), dst_ref=chunk_of(y), send_sem=g_send.at[k], recv_sem=g_recv.at[k],
            device_id=peer, device_id_type=MESH,
        ))
        copies[-1].start()
    pass_on(0, y)
    for k in reversed(far_first(ny)):
        source = lax.rem(y + ny - k, ny)
        pltpu.make_async_copy(chunk_of(source), chunk_of(source), g_recv.at[k]).wait()
        pass_on(k, source)
    for k in range(ny):
        source = lax.rem(y + ny - k, ny)
        theirs = fin.at[pl.ds((1 - core) * count + source * chunk, chunk)]
        pltpu.make_async_copy(theirs, theirs, f_recv.at[k]).wait()
    gram_ref[...] = fin[...]

    for copy in copies:
        copy.wait_send()

    @pl.when(has_low)
    def _():
        for q in range(REACH):
            to_low(q).wait_send()

    @pl.when(has_high)
    def _():
        for q in range(REACH):
            to_high(q).wait_send()

    for j in range(LINES):
        pltpu.make_async_copy(high_v.at[j], high_hbm.at[j], store_sem.at[j]).wait()
        pltpu.make_async_copy(low_v.at[j], low_hbm.at[j], store_sem.at[LINES + j]).wait()


def front(sizes, sketch, marginal_std, cov_tiles, tile_cols):
    rows, k = sketch.shape
    tile = cov_tiles.shape[1]
    ny, nx, nz = sizes["ny"], sizes["nx"], sizes["nzh"] * sizes["nzl"]
    total = rows * sizes["nx"] * ny * nz * 2
    count = 24
    chunk = count // ny
    vmem, dma = pltpu.VMEM, pltpu.SemaphoreType.DMA
    block = (LINES, tile, k)
    scratch = [
        vmem(block, BF16), vmem(cov_tiles.shape, BF16), vmem((2 * REACH + LINES, tile, k), BF16),
        vmem((REACH, tile, k), BF16), vmem((REACH, tile, k), BF16),
        vmem((16, 128), F32), vmem((128, 16), F32), vmem(block, F32), vmem(block, BF16), vmem(block, BF16),
        vmem((k, 2 * k), F32),
        vmem((2 * count, 8, 128), F32), vmem((count, 8, 128), F32), vmem((count, 8, 128), F32),
        vmem((ny, chunk, 8, 128), F32), vmem((chunk, 8, 128), F32), vmem((nz, chunk, 8, 128), F32),
        vmem((chunk, 8, 128), F32), vmem((nx, chunk, 8, 128), F32), vmem((2 * count, 8, 128), F32),
        dma((2,)), dma((2 * LINES,)), dma((2 * REACH,)), dma((2 * REACH,)), dma((1,)), dma((1,)),
        dma((ny,)), dma((ny,)), dma((nz,)), dma((nz,)), dma((nx,)), dma((nx,)),
        dma((ny,)), dma((ny,)), dma((ny,)), dma((ny,)),
    ]
    anywhere = pl.BlockSpec(memory_space=pl.ANY)
    return pl.pallas_call(
        functools.partial(front_kernel, sizes, 1.0 / total),
        out_shape=(
            jax.ShapeDtypeStruct(block, BF16), jax.ShapeDtypeStruct(block, BF16),
            jax.ShapeDtypeStruct((2 * count, 8, 128), F32),
        ),
        in_specs=[pl.BlockSpec(memory_space=pltpu.SMEM), pl.BlockSpec(memory_space=pltpu.VMEM), anywhere, anywhere],
        out_specs=(anywhere, anywhere, pl.BlockSpec(memory_space=pltpu.VMEM)),
        scratch_shapes=scratch,
        compiler_params=pltpu.CompilerParams(collective_id=0, has_side_effects=True, vmem_limit_bytes=48 * 2**20),
        name="front",
    )(tile_cols, marginal_std.reshape(LINES, 2, 128), sketch.reshape(block), cov_tiles)


def split3(a):
    a1 = a.astype(BF16)
    rest = a - a1.astype(F32)
    a2 = rest.astype(BF16)
    return a1, a2, (rest - a2.astype(F32)).astype(BF16)


def factor_in_place(work, rows_w, rows_f, n):
    def panel(p, carry):
        lane = lax.broadcasted_iota(jnp.int32, (8, 128), 1)
        sub = lax.broadcasted_iota(jnp.int32, (8, 128), 0)
        groups = PANEL // 8
        left = [work[8 * g : 8 * g + 8, 0:128] for g in range(groups)]
        right = [work[8 * g : 8 * g + 8, 128:n] for g in range(groups)]
        for m in range(PANEL // PIVOT):
            c0 = m * PIVOT
            g0, s0 = c0 // 8, c0 % 8
            inside = (lane >= c0) & (lane < c0 + PIVOT)
            cols = [[jnp.broadcast_to(left[g][:, c0 + q : c0 + q + 1], (8, 128)) for q in range(PIVOT)]
                    for g in range(g0, groups)]
            pick = lambda r, q: jnp.broadcast_to(cols[0][q][s0 + r : s0 + r + 1, :], (8, 128))
            piv = {(r, q): pick(r, q) for q in range(PIVOT) for r in range(q, PIVOT)}
            row_l = [jnp.broadcast_to(left[g0][s0 + q : s0 + q + 1, :], (8, 128)) for q in range(PIVOT)]
            row_r = [jnp.broadcast_to(right[g0][s0 + q : s0 + q + 1, :], (8, 128)) for q in range(PIVOT)]
            row_l = [jnp.where(inside, jnp.where(lane == c0 + q, 1.0, 0.0), row_l[q]) for q in range(PIVOT)]
            u = {}
            inv = []
            for q in range(PIVOT):
                d = piv[q, q]
                i = lax.rsqrt(d)
                inv.append(i)
                u[q, q] = d * i
                for r in range(q + 1, PIVOT):
                    u[q, r] = piv[r, q] * i
                for r in range(q + 1, PIVOT):
                    for t in range(r, PIVOT):
                        piv[t, r] = piv[t, r] - u[q, r] * u[q, t]

            def sweep(v):
                out = []
                for q in range(PIVOT):
                    a = v[q]
                    for r in range(q):
                        a = a - u[r, q] * out[r]
                    out.append(a * inv[q])
                return out

            z_l, z_r = sweep(row_l), sweep(row_r)
            for q in range(PIVOT):
                row = pl.ds(c0 + q, 1)
                rows_w[p, row, 0:128] = z_l[q][0:1]
                rows_w[p, row, 128:n] = z_r[q][0:1]
                f = jnp.where(inside, 0.0, z_l[q])
                for r in range(q, PIVOT):
                    f = jnp.where(lane == c0 + r, u[q, r], f)
                rows_f[p, row, 0:128] = f[0:1]
                rows_f[p, row, 128:n] = z_r[q][0:1]
            for g in range(g0, groups):
                if g == g0 and s0 + PIVOT == 8:
                    continue
                w = sweep(cols[g - g0])
                if g == g0:
                    w = [jnp.where(sub >= s0 + PIVOT, v, 0.0) for v in w]
                cleared = jnp.where(inside & (sub >= s0 + PIVOT) if g == g0 else inside, 0.0, left[g])
                for q in range(PIVOT):
                    cleared = cleared - w[q] * z_l[q]
                    right[g] = right[g] - w[q] * z_r[q]
                left[g] = cleared

        at = lax.broadcasted_iota(jnp.int32, (PANEL, n), 1)
        below_diagonal = at <= lax.broadcasted_iota(jnp.int32, (PANEL, n), 0)
        b1, b2, b3 = split3(jnp.where(below_diagonal | (at >= PANEL), rows_w[p], 0.0))
        lhs = jnp.concatenate([b1, b1, b2, b2, b1, b3], axis=0)
        rhs = jnp.concatenate([b1, b2, b1, b2, b3, b1], axis=0)
        update = lax.dot_general(lhs, rhs, (((0,), (0,)), ((), ())), preferred_element_type=F32)
        lanes = lax.broadcasted_iota(jnp.int32, (n - PANEL, n), 1)
        fresh = jnp.where(lanes < PANEL, 0.0, work[PANEL:, :]) - update[PANEL:, :]
        work[0 : n - PANEL, :] = pltpu.roll(fresh, n - PANEL, 1)
        return carry

    lax.fori_loop(0, n // PANEL, panel, 0)


def back_kernel(cols_ref, gram_ref, high_hbm, low_hbm, basis_hbm, factor_ref,
                high_v, low_v, out_v, work, rows_w, rows_f, w_high, w_low, load_sem, out_sem):
    n = work.shape[0]
    half = n // 2
    loads = [
        pltpu.make_async_copy(high_hbm, high_v, load_sem.at[0]),
        pltpu.make_async_copy(low_hbm, low_v, load_sem.at[1]),
    ]
    for copy in loads:
        copy.start()
    upper = gram_ref[16:32].reshape(half, half)
    work[0:half, 0:half] = gram_ref[0:16].reshape(half, half)
    work[0:half, half:] = upper
    work[half:, 0:half] = upper.T
    work[half:, half:] = gram_ref[32:48].reshape(half, half)
    factor_in_place(work, rows_w, rows_f, n)

    for p in range(n // PANEL):
        rows = slice(p * PANEL, p * PANEL + PANEL)
        row = lax.broadcasted_iota(jnp.int32, (PANEL, n), 0) + p * PANEL
        col = lax.broadcasted_iota(jnp.int32, (PANEL, n), 1)
        w, f = rows_w[p], rows_f[p]
        if p:
            w, f = pltpu.roll(w, p * PANEL, 1), pltpu.roll(f, p * PANEL, 1)
        w = jnp.where(col <= row, w, 0.0)
        factor_ref[rows, :] = jnp.where(col >= row, f, 0.0)
        high = w.astype(BF16)
        w_high[rows, :] = high
        w_low[rows, :] = (w - high.astype(F32)).astype(BF16)

    for copy in loads:
        copy.wait()
    wh, wl = w_high[...], w_low[...]
    weights = jnp.concatenate([wh, wl, wh], axis=1)
    writes = []
    for t in range(LINES):
        head = t // REACH * REACH
        start = cols_ref[head, REACH]
        start = start - start % REACH
        line = jnp.int32(head)
        for e in range(REACH):
            line += jnp.where(cols_ref[t, e] >= start, 1, 0)
        line = jnp.clip(line, 0, LINES - 1)
        h, l = high_v[line], low_v[line]
        out_v[t] = lax.dot_general(
            jnp.concatenate([h, h, l], axis=1), weights, (((1,), (1,)), ((), ())), preferred_element_type=F32
        )
        writes.append(pltpu.make_async_copy(out_v.at[t], basis_hbm.at[t], out_sem.at[t]))
        writes[-1].start()
    for copy in writes:
        copy.wait()


def back(tile_cols, gram, high, low):
    lines, tile, k = high.shape
    vmem, dma = pltpu.VMEM, pltpu.SemaphoreType.DMA
    anywhere = pl.BlockSpec(memory_space=pl.ANY)
    in_vmem = pl.BlockSpec(memory_space=pltpu.VMEM)
    return pl.pallas_call(
        back_kernel,
        out_shape=(jax.ShapeDtypeStruct((lines, tile, k), F32), jax.ShapeDtypeStruct((k, k), F32)),
        in_specs=[pl.BlockSpec(memory_space=pltpu.SMEM), in_vmem, anywhere, anywhere],
        out_specs=(anywhere, in_vmem),
        scratch_shapes=[
            vmem((lines, tile, k), BF16), vmem((lines, tile, k), BF16), vmem((lines, tile, k), F32),
            vmem((k, k), F32), vmem((k // PANEL, PANEL, k), F32), vmem((k // PANEL, PANEL, k), F32),
            vmem((k, k), BF16), vmem((k, k), BF16), dma((2,)), dma((lines,)),
        ],
        compiler_params=pltpu.CompilerParams(vmem_limit_bytes=48 * 2**20),
        name="back",
    )(tile_cols, gram, high, low)


def per_device(sizes, sketch, marginal_std, cov_tiles, tile_cols):
    high, low, gram = front(sizes, sketch, marginal_std, cov_tiles, tile_cols)
    basis, factor = back(tile_cols, gram, high, low)
    return basis.reshape(sketch.shape), factor


def build(mesh, sizes):
    in_specs = (P(("grp", "dev"), None), P(("grp", "dev")), P(), P(("grp", "dev"), None))
    out_specs = (P(("grp", "dev"), None), P())
    return jax.shard_map(
        functools.partial(per_device, sizes), mesh=mesh, in_specs=in_specs, out_specs=out_specs, check_vma=False
    )


def solution(mesh):
    return build(mesh, SIZES)
```

time: 431 us -> 74.9 us (0.17)
  waiting for transfers between devices: 298 us -> 0 us
  Pallas kernels: 0 us -> 70.1 us
  other arithmetic: 67.5 us -> 0 us
  matrix products: 17.9 us -> 0 us
  local copies, waits for them, and re-layouts: 20.7 us -> 3.87 us
  between operations: 15.6 us -> 0.65 us
  starting transfers between devices: 10.1 us -> 0 us
    psum x1 -> x0, waiting for transfers between devices: 269 us -> none  [per_device(): gram_matrix = lax.psum(gram_matrix, ('grp', 'dev'))]
    pallas_call x0 -> x2, Pallas kernels: none -> 70.1 us  [the longest x1 53.8 us: front(): pl.pallas_call(functools.partial(front_kernel, sizes, 1.0 / total), out_s...]
    another operation x9 -> x0, other arithmetic: 58.4 us -> none  [the longest x6 37.2 us: per_device(): lower_factor = jnp.linalg.cholesky(gram_matrix)]
    ppermute x2 -> x0, waiting for transfers between devices: 29.4 us -> none  [the longest x1 20.8 us: with_halo(): lax.ppermute(lax.slice_in_dim(block, 0, width, axis=dim), axis, backward)]
    dot_general x2 -> x0, matrix products: 10.3 us -> none  [the longest x1 5.46 us: per_device(): jnp.einsum('eij,etjk->tik', cov_tiles, gathered, preferred_element_type=j...]
    ppermute x2 -> x0, starting transfers between devices: 10.1 us -> none  [the longest x1 7.19 us: with_halo(): lax.ppermute(lax.slice_in_dim(block, block.shape[dim] - width, None, axis...]
    gather x1 -> x0, local copies, waits for them, and re-layouts: 7.83 us -> none  [per_device(): gathered = extended_tiles[local_cols.T]]
    another operation x5 -> x0, matrix products: 7.65 us -> none  [the longest x3 4.83 us: per_device(): lax.linalg.triangular_solve(lower_factor, latent_field, left_side=False,...]
  transfers between devices with their start and end apart: 3 -> 0, of which waited for: 3 -> 0; matrix products, arithmetic and copies ran while one was open for 1% -> 0% of each run, Pallas kernels for 0% -> 0%
where the time goes in v1:
time: 74.9 us; the launch traced here: 74.7 us
  Pallas kernels  70.1 us (94%)
  local copies, waits for them, and re-layouts  3.87 us (5%)
    pallas_call x1, Pallas kernels, front(): pl.pallas_call(functools.partial(front_kernel, sizes, 1.0 / total), out_s...  53.8 us
    pallas_call x1, Pallas kernels, back(): pl.pallas_call(back_kernel, out_shape=(jax.ShapeDtypeStruct((lines, tile,...  16.3 us
    unnamed x8, local copies, waits for them, and re-layouts  3.87 us

profile of v1, /device:TPU:1, one launch (start us, length us, event | category | flops | bytes accessed | tf_op | source)
XLA Modules:
  0.0 74.7 jit_solution(15770911839225910322)
XLA Ops:
  0.6 0.0 copy-start
  0.6 1.3 %copy-done = bf16[9,256,256]{2,1,0:T(8,128)(2,1)S(1)} copy-done((bf16[9,256,256]{2,1,0:T(8,128)(2,1)S(1)}, bf16[9,256,256]{2,1,0:T(8,128)(2,1)}, u32[]{:S(2)}) %copy-start) | copy-done | bytes 1179672
  1.9 0.0 copy-start.1
  1.9 1.2 %copy-done.1 = bf16[2048,256]{1,0:T(8,128)(2,1)S(1)} copy-done((bf16[2048,256]{1,0:T(8,128)(2,1)S(1)}, bf16[2048,256]{1,0:T(8,128)(2,1)}, u32[]{:S(2)}) %copy-start.1) | copy-done | bytes 1048600
  3.1 0.0 copy-start.2
  3.1 0.7 copy-done.2
  3.8 0.0 copy-start.3
  3.8 0.7 copy-done.3
  4.5 53.8 %front.1 = (bf16[8,256,256]{2,1,0:T(8,128)(2,1)S(1)}, bf16[8,256,256]{2,1,0:T(8,128)(2,1)S(1)}, f32[48,8,128]{2,1,0:T(8,128)S(1)}) custom-call(s32[8,9]{1,0:T(8,128)S(1)} %copy-done.2, f32[8,2,128]{2,1,0:T(2,128)S(1)} %bitcast.4, bf16[8,256,256]{2,1,0:T(8,128)(2,1)S(1)} %bitcast.3, bf16[9,256,256]{2,1,0:T(8,128)(2,1)S(1)} %copy-done), custom_call_target="tpu_custom_call" | custom-call | tf_op jit(solution)/shard_map/front/pallas_call | solution.py:297
  58.3 16.3 %back.1 = (f32[8,256,256]{2,1,0:T(8,128)}, f32[256,256]{1,0:T(8,128)}) custom-call(s32[8,9]{1,0:T(8,128)S(1)} %copy-done.2, f32[48,8,128]{2,1,0:T(8,128)S(1)} %get-tuple-element.7.gram_ref, bf16[8,256,256]{2,1,0:T(8,128)(2,1)S(1)} %get-tuple-element.8.high_hbm, bf16[8,256,256]{2,1,0:T(8,128)(2,1)S(1)} %get-tuple-element.9.low_hbm), custom_call_target="tpu_custom_call" | custom-call | tf_op jit(solution)/shard_map/back/pallas_call | solution.py:452
Async XLA Ops:
  0.6 1.3 %copy-start = (bf16[9,256,256]{2,1,0:T(8,128)(2,1)S(1)}, bf16[9,256,256]{2,1,0:T(8,128)(2,1)}, u32[]{:S(2)}) copy-start(bf16[9,256,256]{2,1,0:T(8,128)(2,1)} %cov_hbm.1) | copy-start | bytes 3538948
  1.9 1.2 %copy-start.1 = (bf16[2048,256]{1,0:T(8,128)(2,1)S(1)}, bf16[2048,256]{1,0:T(8,128)(2,1)}, u32[]{:S(2)}) copy-start(bf16[2048,256]{1,0:T(8,128)(2,1)} %param.4) | copy-start | bytes 3145732
  3.1 0.7 copy-start.2
  3.8 0.7 copy-start.3

commit v2 on v1

--- a/solution.py
+++ b/solution.py
@@ -13,9 +13,13 @@
 LINES = 8
 LAGS = 9
 PANEL = 32
-PIVOT = 4
+PIVOT = 8
 
 SIZES = dict(nx=4, ny=8, nzh=4, nzl=2)
+
+
+def pin_hbm(a):
+    return pltpu.with_memory_space_constraint(a, pltpu.HBM)
 
 
 def far_first(n):
@@ -23,11 +27,11 @@
 
 
 def front_kernel(
-    sizes, scale, cols_ref, std_ref, sketch_hbm, cov_hbm, high_hbm, low_hbm, gram_ref,
-    sketch_v, cov_v, own, below, above, std_sorted, std_cols, acc, high_v, low_v, gacc,
-    packed, from_core, part_y, got_y, sum_y, got_z, sum_z, got_x, fin,
-    load_sem, store_sem, halo_send, halo_recv, core_send, core_recv, y_send, y_recv,
-    z_send, z_recv, x_send, x_recv, g_send, g_recv, f_send, f_recv,
+    sizes, scale, cols_hbm, std_hbm, sketch_hbm, cov_hbm, high_v, low_v, fin,
+    cols_ref, std_ref, sketch_v, cov_v, own, below, above, std_sorted, std_cols, acc, gacc,
+    packed, from_core, part, got_a, sum_a, got_b, sum_b, got_x,
+    load_sem, halo_send, halo_recv, core_send, core_recv, a_send, a_recv,
+    b_send, b_recv, x_send, x_recv, g_send, g_recv, f_send, f_recv,
 ):
     nx, ny, nzh, nzl = sizes["nx"], sizes["ny"], sizes["nzh"], sizes["nzl"]
     nz = nzh * nzl
@@ -51,10 +55,12 @@
     has_outer = (outer >= 0) & (outer < total)
     has_low, has_high = me > 0, me < total - 1
 
-    load_sketch = pltpu.make_async_copy(sketch_hbm, sketch_v, load_sem.at[0])
-    load_cov = pltpu.make_async_copy(cov_hbm, cov_v, load_sem.at[1])
-    load_sketch.start()
-    load_cov.start()
+    load_cols = pltpu.make_async_copy(cols_hbm, cols_ref, load_sem.at[0])
+    load_std = pltpu.make_async_copy(std_hbm, std_ref, load_sem.at[1])
+    load_sketch = pltpu.make_async_copy(sketch_hbm, sketch_v, load_sem.at[2])
+    load_cov = pltpu.make_async_copy(cov_hbm, cov_v, load_sem.at[3])
+    for copy in (load_cols, load_std, load_sketch, load_cov):
+        copy.start()
 
     barrier = pltpu.get_barrier_semaphore()
 
@@ -72,6 +78,20 @@
     def _():
         greet(linear(outer))
 
+    gacc[...] = jnp.zeros_like(gacc)
+    zero_lines = jnp.zeros((REACH,) + own.shape[1:], BF16)
+    own[0:REACH] = zero_lines
+    own[REACH + LINES :] = zero_lines
+
+    @pl.when(jnp.logical_not(has_low))
+    def _():
+        below[...] = zero_lines
+
+    @pl.when(jnp.logical_not(has_high))
+    def _():
+        above[...] = zero_lines
+
+    load_cols.wait()
     tile_of_line = []
     for block in range(LINES // REACH):
         head = block * REACH
@@ -83,18 +103,7 @@
             tile = cols_ref[head, REACH - offset + j] - start
             tile_of_line.append(jnp.clip(tile, 0, REACH - 1) + head)
 
-    zero_lines = jnp.zeros((REACH,) + own.shape[1:], BF16)
-    own[0:REACH] = zero_lines
-    own[REACH + LINES :] = zero_lines
-
-    @pl.when(jnp.logical_not(has_low))
-    def _():
-        below[...] = zero_lines
-
-    @pl.when(jnp.logical_not(has_high))
-    def _():
-        above[...] = zero_lines
-
+    load_std.wait()
     for j in range(LINES):
         std_sorted[2 * j : 2 * j + 2, :] = std_ref[tile_of_line[j]]
     std_cols[...] = std_sorted[...].T
@@ -105,7 +114,16 @@
     load_sketch.wait()
     for j in (0, 7, 1, 6, 2, 5, 3, 4):
         own[REACH + j] = (sketch_v[tile_of_line[j]].astype(F32) * std_of(j)).astype(BF16)
-    gacc[...] = jnp.zeros_like(gacc)
+
+    n, a_at, b_at = ny, jnp.where(core == 0, y, z), jnp.where(core == 0, z, y)
+
+    def cross(first, second):
+        return [
+            (k, tuple(jnp.where(core == 0, p, q) for p, q in zip(one, two)))
+            for (k, one), (_, two) in zip(first, second)
+        ]
+
+    a_peers, b_peers = cross(y_peers, z_peers), cross(z_peers, y_peers)
 
     peers = len(y_peers) + len(z_peers) + len(x_peers) + 1
     pl.semaphore_wait(barrier, peers + jnp.where(has_outer, 1, 0))
@@ -150,8 +168,6 @@
         low_v[j] = low
         pair = jnp.concatenate([high, low], axis=1)
         gacc[...] += lax.dot_general(high, pair, (((0,), (0,)), ((), ())), preferred_element_type=F32)
-        pltpu.make_async_copy(high_v.at[j], high_hbm.at[j], store_sem.at[j]).start()
-        pltpu.make_async_copy(low_v.at[j], low_hbm.at[j], store_sem.at[LINES + j]).start()
 
     for q in range(REACH):
         @pl.when(has_low)
@@ -179,11 +195,11 @@
                 acc[j] = product
 
     half = gacc.shape[0] // 2
-    for n, (r, c) in enumerate(((0, 0), (0, half), (half, half))):
+    for block, (r, c) in enumerate(((0, 0), (0, half), (half, half))):
         hh = gacc[r : r + half, c : c + half]
         hl = gacc[r : r + half, 2 * half + c : 3 * half + c]
         lh = gacc[c : c + half, 2 * half + r : 3 * half + r].T
-        packed[16 * n : 16 * n + 16] = ((hh + (hl + lh)) * scale).reshape(16, 8, 128)
+        packed[16 * block : 16 * block + 16] = ((hh + (hl + lh)) * scale).reshape(16, 8, 128)
 
     count = packed.shape[0] // 2
     chunk = count // ny
@@ -193,19 +209,19 @@
     )
     swap.start()
     swap.wait()
-    part_y[...] = packed[pl.ds(core * count, count)] + from_core[...]
+    part[...] = packed[pl.ds(core * count, count)] + from_core[...]
 
     copies = []
-    for k, peer in y_peers:
+    for k, peer in a_peers:
         copies.append(pltpu.make_async_remote_copy(
-            src_ref=part_y.at[pl.ds(lax.rem(y + k, ny) * chunk, chunk)], dst_ref=got_y.at[k],
-            send_sem=y_send.at[k], recv_sem=y_recv.at[k], device_id=peer, device_id_type=MESH,
+            src_ref=part.at[pl.ds(lax.rem(a_at + k, n) * chunk, chunk)], dst_ref=got_a.at[k],
+            send_sem=a_send.at[k], recv_sem=a_recv.at[k], device_id=peer, device_id_type=MESH,
         ))
         copies[-1].start()
-    value = part_y[pl.ds(y * chunk, chunk)]
-    for k in range(1, ny):
-        pltpu.make_async_copy(got_y.at[k], got_y.at[k], y_recv.at[k]).wait()
-        value = value + got_y[k]
+    value = part[pl.ds(a_at * chunk, chunk)]
+    for k in reversed(far_first(n)):
+        pltpu.make_async_copy(got_a.at[k], got_a.at[k], a_recv.at[k]).wait()
+        value = value + got_a[k]
 
     def gather_sum(value, here, n, peers_, source, slots, send, recv):
         source[...] = value
@@ -223,37 +239,35 @@
             out = out + slots[i]
         return out
 
-    value = gather_sum(value, z, nz, z_peers, sum_y, got_z, z_send, z_recv)
-    value = gather_sum(value, x, nx, x_peers, sum_z, got_x, x_send, x_recv)
-
-    def chunk_of(y_):
-        return fin.at[pl.ds(core * count + y_ * chunk, chunk)]
-
-    def pass_on(k, y_):
+    value = gather_sum(value, b_at, n, b_peers, sum_a, got_b, b_send, b_recv)
+    value = gather_sum(value, x, nx, x_peers, sum_b, got_x, x_send, x_recv)
+
+    def chunk_of(a_):
+        return fin.at[pl.ds(core * count + a_ * chunk, chunk)]
+
+    def pass_on(k, a_):
         copies.append(pltpu.make_async_remote_copy(
-            src_ref=chunk_of(y_), dst_ref=chunk_of(y_), send_sem=f_send.at[k], recv_sem=f_recv.at[k],
+            src_ref=chunk_of(a_), dst_ref=chunk_of(a_), send_sem=f_send.at[k], recv_sem=f_recv.at[k],
             device_id=mate, device_id_type=MESH,
         ))
         copies[-1].start()
 
-    fin[pl.ds(core * count + y * chunk, chunk)] = value
-    for k, peer in y_peers:
+    fin[pl.ds(core * count + a_at * chunk, chunk)] = value
+    for k, peer in a_peers:
         copies.append(pltpu.make_async_remote_copy(
-            src_ref=chunk_of(y), dst_ref=chunk_of(y), send_sem=g_send.at[k], recv_sem=g_recv.at[k],
+            src_ref=chunk_of(a_at), dst_ref=chunk_of(a_at), send_sem=g_send.at[k], recv_sem=g_recv.at[k],
             device_id=peer, device_id_type=MESH,
         ))
         copies[-1].start()
-    pass_on(0, y)
-    for k in reversed(far_first(ny)):
-        source = lax.rem(y + ny - k, ny)
+    pass_on(0, a_at)
+    for k in reversed(far_first(n)):
+        source = lax.rem(a_at + n - k, n)
         pltpu.make_async_copy(chunk_of(source), chunk_of(source), g_recv.at[k]).wait()
         pass_on(k, source)
-    for k in range(ny):
-        source = lax.rem(y + ny - k, ny)
+    for k in range(n):
+        source = lax.rem(b_at + n - k, n)
         theirs = fin.at[pl.ds((1 - core) * count + source * chunk, chunk)]
         pltpu.make_async_copy(theirs, theirs, f_recv.at[k]).wait()
-    gram_ref[...] = fin[...]
-
     for copy in copies:
         copy.wait_send()
 
@@ -266,10 +280,6 @@
     def _():
         for q in range(REACH):
             to_high(q).wait_send()
-
-    for j in range(LINES):
-        pltpu.make_async_copy(high_v.at[j], high_hbm.at[j], store_sem.at[j]).wait()
-        pltpu.make_async_copy(low_v.at[j], low_hbm.at[j], store_sem.at[LINES + j]).wait()
 
 
 def front(sizes, sketch, marginal_std, cov_tiles, tile_cols):
@@ -282,30 +292,31 @@
     vmem, dma = pltpu.VMEM, pltpu.SemaphoreType.DMA
     block = (LINES, tile, k)
     scratch = [
-        vmem(block, BF16), vmem(cov_tiles.shape, BF16), vmem((2 * REACH + LINES, tile, k), BF16),
+        pltpu.SMEM(tile_cols.shape, jnp.int32), vmem((LINES, 2, 128), F32), vmem(block, BF16), vmem(cov_tiles.shape, BF16), vmem((2 * REACH + LINES, tile, k), BF16),
         vmem((REACH, tile, k), BF16), vmem((REACH, tile, k), BF16),
-        vmem((16, 128), F32), vmem((128, 16), F32), vmem(block, F32), vmem(block, BF16), vmem(block, BF16),
+        vmem((16, 128), F32), vmem((128, 16), F32), vmem(block, F32),
         vmem((k, 2 * k), F32),
         vmem((2 * count, 8, 128), F32), vmem((count, 8, 128), F32), vmem((count, 8, 128), F32),
         vmem((ny, chunk, 8, 128), F32), vmem((chunk, 8, 128), F32), vmem((nz, chunk, 8, 128), F32),
-        vmem((chunk, 8, 128), F32), vmem((nx, chunk, 8, 128), F32), vmem((2 * count, 8, 128), F32),
-        dma((2,)), dma((2 * LINES,)), dma((2 * REACH,)), dma((2 * REACH,)), dma((1,)), dma((1,)),
+        vmem((chunk, 8, 128), F32), vmem((nx, chunk, 8, 128), F32),
+        dma((4,)), dma((2 * REACH,)), dma((2 * REACH,)), dma((1,)), dma((1,)),
         dma((ny,)), dma((ny,)), dma((nz,)), dma((nz,)), dma((nx,)), dma((nx,)),
         dma((ny,)), dma((ny,)), dma((ny,)), dma((ny,)),
     ]
-    anywhere = pl.BlockSpec(memory_space=pl.ANY)
+    in_hbm = pl.BlockSpec(memory_space=pltpu.HBM)
+    in_vmem = pl.BlockSpec(memory_space=pltpu.VMEM)
     return pl.pallas_call(
         functools.partial(front_kernel, sizes, 1.0 / total),
         out_shape=(
             jax.ShapeDtypeStruct(block, BF16), jax.ShapeDtypeStruct(block, BF16),
             jax.ShapeDtypeStruct((2 * count, 8, 128), F32),
         ),
-        in_specs=[pl.BlockSpec(memory_space=pltpu.SMEM), pl.BlockSpec(memory_space=pltpu.VMEM), anywhere, anywhere],
-        out_specs=(anywhere, anywhere, pl.BlockSpec(memory_space=pltpu.VMEM)),
+        in_specs=[in_hbm] * 4,
+        out_specs=(in_vmem,) * 3,
         scratch_shapes=scratch,
         compiler_params=pltpu.CompilerParams(collective_id=0, has_side_effects=True, vmem_limit_bytes=48 * 2**20),
         name="front",
-    )(tile_cols, marginal_std.reshape(LINES, 2, 128), sketch.reshape(block), cov_tiles)
+    )(*(pin_hbm(a) for a in (tile_cols, marginal_std.reshape(LINES, 2, 128), sketch.reshape(block), cov_tiles)))
 
 
 def split3(a):
@@ -391,16 +402,12 @@
     lax.fori_loop(0, n // PANEL, panel, 0)
 
 
-def back_kernel(cols_ref, gram_ref, high_hbm, low_hbm, basis_hbm, factor_ref,
-                high_v, low_v, out_v, work, rows_w, rows_f, w_high, w_low, load_sem, out_sem):
+def back_kernel(cols_hbm, gram_ref, high_v, low_v, basis_hbm, factor_ref,
+                cols_ref, out_v, work, rows_w, rows_f, w_high, w_low, load_sem, out_sem):
     n = work.shape[0]
     half = n // 2
-    loads = [
-        pltpu.make_async_copy(high_hbm, high_v, load_sem.at[0]),
-        pltpu.make_async_copy(low_hbm, low_v, load_sem.at[1]),
-    ]
-    for copy in loads:
-        copy.start()
+    load_cols = pltpu.make_async_copy(cols_hbm, cols_ref, load_sem.at[0])
+    load_cols.start()
     upper = gram_ref[16:32].reshape(half, half)
     work[0:half, 0:half] = gram_ref[0:16].reshape(half, half)
     work[0:half, half:] = upper
@@ -421,8 +428,7 @@
         w_high[rows, :] = high
         w_low[rows, :] = (w - high.astype(F32)).astype(BF16)
 
-    for copy in loads:
-        copy.wait()
+    load_cols.wait()
     wh, wl = w_high[...], w_low[...]
     weights = jnp.concatenate([wh, wl, wh], axis=1)
     writes = []
@@ -447,21 +453,21 @@
 def back(tile_cols, gram, high, low):
     lines, tile, k = high.shape
     vmem, dma = pltpu.VMEM, pltpu.SemaphoreType.DMA
-    anywhere = pl.BlockSpec(memory_space=pl.ANY)
+    in_hbm = pl.BlockSpec(memory_space=pltpu.HBM)
     in_vmem = pl.BlockSpec(memory_space=pltpu.VMEM)
     return pl.pallas_call(
         back_kernel,
         out_shape=(jax.ShapeDtypeStruct((lines, tile, k), F32), jax.ShapeDtypeStruct((k, k), F32)),
-        in_specs=[pl.BlockSpec(memory_space=pltpu.SMEM), in_vmem, anywhere, anywhere],
-        out_specs=(anywhere, in_vmem),
+        in_specs=[in_hbm, in_vmem, in_vmem, in_vmem],
+        out_specs=(in_hbm, in_vmem),
         scratch_shapes=[
-            vmem((lines, tile, k), BF16), vmem((lines, tile, k), BF16), vmem((lines, tile, k), F32),
+            pltpu.SMEM(tile_cols.shape, jnp.int32), vmem((lines, tile, k), F32),
             vmem((k, k), F32), vmem((k // PANEL, PANEL, k), F32), vmem((k // PANEL, PANEL, k), F32),
-            vmem((k, k), BF16), vmem((k, k), BF16), dma((2,)), dma((lines,)),
+            vmem((k, k), BF16), vmem((k, k), BF16), dma((1,)), dma((lines,)),
         ],
         compiler_params=pltpu.CompilerParams(vmem_limit_bytes=48 * 2**20),
         name="back",
-    )(tile_cols, gram, high, low)
+    )(pin_hbm(tile_cols), gram, high, low)
 
 
 def per_device(sizes, sketch, marginal_std, cov_tiles, tile_cols):

time: 74.9 us -> 63.9 us (0.85)
  Pallas kernels: 70.1 us -> 63.1 us
  local copies, waits for them, and re-layouts: 3.87 us -> 0 us
    pallas_call x1, Pallas kernels: 16.3 us -> 12 us  [back(): pl.pallas_call(back_kernel, out_shape=(jax.ShapeDtypeStruct((lines, tile,...]
    unnamed x8 -> x0, local copies, waits for them, and re-layouts: 3.87 us -> none
    pallas_call x1, Pallas kernels: 53.8 us -> 51.1 us  [front(): pl.pallas_call(functools.partial(front_kernel, sizes, 1.0 / total), out_s...]
where the time goes in v2:
time: 63.9 us; the launch traced here: 63.7 us
  Pallas kernels  63.1 us (99%)
  between operations  0.64 us (1%)
    pallas_call x1, Pallas kernels, front(): pl.pallas_call(functools.partial(front_kernel, sizes, 1.0 / total), out_s...  51.1 us
    pallas_call x1, Pallas kernels, back(): pl.pallas_call(back_kernel, out_shape=(jax.ShapeDtypeStruct((lines, tile,...  12 us

profile of v2, /device:TPU:1, one launch (start us, length us, event | category | flops | bytes accessed | tf_op | source)
XLA Modules:
  0.0 63.7 jit_solution(9116890066506783400)
XLA Ops:
  0.6 51.1 %front.1 = (bf16[8,256,256]{2,1,0:T(8,128)(2,1)S(1)}, bf16[8,256,256]{2,1,0:T(8,128)(2,1)S(1)}, f32[48,8,128]{2,1,0:T(8,128)S(1)}) custom-call(s32[8,9]{1,0:T(8,128)} %cols_hbm.3, f32[8,2,128]{2,1,0:T(2,128)} %bitcast.4, bf16[8,256,256]{2,1,0:T(8,128)(2,1)} %bitcast.3, bf16[9,256,256]{2,1,0:T(8,128)(2,1)} %cov_hbm.1), custom_call_target="tpu_custom_call" | custom-call | tf_op jit(solution)/shard_map/front/pallas_call | solution.py:308
  51.7 12.0 %back.1 = (f32[8,256,256]{2,1,0:T(8,128)}, f32[256,256]{1,0:T(8,128)}) custom-call(s32[8,9]{1,0:T(8,128)} %cols_hbm.3, f32[48,8,128]{2,1,0:T(8,128)S(1)} %get-tuple-element.7.gram_ref, bf16[8,256,256]{2,1,0:T(8,128)(2,1)S(1)} %get-tuple-element.8.high_v, bf16[8,256,256]{2,1,0:T(8,128)(2,1)S(1)} %get-tuple-element.9.low_v), custom_call_target="tpu_custom_call" | custom-call | tf_op jit(solution)/shard_map/back/pallas_call | solution.py:458

commit v3 on v2

--- a/solution.py
+++ b/solution.py
@@ -29,9 +29,9 @@
 def front_kernel(
     sizes, scale, cols_hbm, std_hbm, sketch_hbm, cov_hbm, high_v, low_v, fin,
     cols_ref, std_ref, sketch_v, cov_v, own, below, above, std_sorted, std_cols, acc, gacc,
-    packed, from_core, part, got_a, sum_a, got_b, sum_b, got_x,
-    load_sem, halo_send, halo_recv, core_send, core_recv, a_send, a_recv,
-    b_send, b_recv, x_send, x_recv, g_send, g_recv, f_send, f_recv,
+    packed, got_a, sum_a, got_b, sum_b, got_x,
+    load_sem, halo_send, halo_recv, a_send, a_recv,
+    b_send, b_recv, x_send, x_recv, g_send, g_recv,
 ):
     nx, ny, nzh, nzl = sizes["nx"], sizes["ny"], sizes["nzh"], sizes["nzl"]
     nz = nzh * nzl
@@ -50,7 +50,6 @@
     def linear(i):
         return (lax.div(i, per_grp), lax.rem(i, per_grp))
 
-    mate = place(x, y, z, 1 - core)
     outer = jnp.where(core == 0, me - 1, me + 1)
     has_outer = (outer >= 0) & (outer < total)
     has_low, has_high = me > 0, me < total - 1
@@ -70,9 +69,10 @@
     y_peers = [(k, place(x, lax.rem(y + k, ny), z, core)) for k in far_first(ny)]
     z_peers = [(k, place(x, y, lax.rem(z + k, nz), core)) for k in far_first(nz)]
     x_peers = [(k, place(lax.rem(x + k, nx), y, z, core)) for k in far_first(nx)]
-    for _, peer in z_peers + y_peers + x_peers:
+    y_across = [(k, place(x, lax.rem(y + k, ny), z, 1 - core)) for k in far_first(ny) + [0]]
+    z_across = [(k, place(x, y, lax.rem(z + k, nz), 1 - core)) for k in far_first(nz) + [0]]
+    for _, peer in z_peers + y_peers + x_peers + y_across + z_across[:-1]:
         greet(peer)
-    greet(mate)
 
     @pl.when(has_outer)
     def _():
@@ -111,9 +111,13 @@
     def std_of(j):
         return jnp.concatenate([std_cols[:, 2 * j : 2 * j + 1], std_cols[:, 2 * j + 1 : 2 * j + 2]], axis=0)
 
+    def scale_lines(q):
+        for j in (q, LINES - 1 - q):
+            own[REACH + j] = (sketch_v[tile_of_line[j]].astype(F32) * std_of(j)).astype(BF16)
+
     load_sketch.wait()
-    for j in (0, 7, 1, 6, 2, 5, 3, 4):
-        own[REACH + j] = (sketch_v[tile_of_line[j]].astype(F32) * std_of(j)).astype(BF16)
+    scale_lines(0)
+    scale_lines(1)
 
     n, a_at, b_at = ny, jnp.where(core == 0, y, z), jnp.where(core == 0, z, y)
 
@@ -124,8 +128,9 @@
         ]
 
     a_peers, b_peers = cross(y_peers, z_peers), cross(z_peers, y_peers)
-
-    peers = len(y_peers) + len(z_peers) + len(x_peers) + 1
+    a_across, b_across = cross(y_across, z_across), cross(z_across, y_across)
+
+    peers = len(z_peers + y_peers + x_peers + y_across + z_across) - 1
     pl.semaphore_wait(barrier, peers + jnp.where(has_outer, 1, 0))
 
     def to_low(q):
@@ -140,15 +145,17 @@
             recv_sem=halo_recv.at[REACH + q], device_id=linear(me + 1), device_id_type=MESH,
         )
 
-    @pl.when(has_low)
-    def _():
-        for q in range(REACH):
+    for q in range(REACH):
+        @pl.when(has_low)
+        def _():
             to_low(q).start()
 
-    @pl.when(has_high)
-    def _():
-        for q in range(REACH):
+        @pl.when(has_high)
+        def _():
             to_high(q).start()
+
+        if q + 2 < REACH:
+            scale_lines(q + 2)
 
     load_cov.wait()
 
@@ -202,72 +209,58 @@
         packed[16 * block : 16 * block + 16] = ((hh + (hl + lh)) * scale).reshape(16, 8, 128)
 
     count = packed.shape[0] // 2
-    chunk = count // ny
-    swap = pltpu.make_async_remote_copy(
-        src_ref=packed.at[pl.ds((1 - core) * count, count)], dst_ref=from_core, send_sem=core_send.at[0],
-        recv_sem=core_recv.at[0], device_id=mate, device_id_type=MESH,
-    )
-    swap.start()
-    swap.wait()
-    part[...] = packed[pl.ds(core * count, count)] + from_core[...]
-
+    chunk = count // n
     copies = []
-    for k, peer in a_peers:
+
+    def send(source, target, send_sem, recv_sem, peer):
         copies.append(pltpu.make_async_remote_copy(
-            src_ref=part.at[pl.ds(lax.rem(a_at + k, n) * chunk, chunk)], dst_ref=got_a.at[k],
-            send_sem=a_send.at[k], recv_sem=a_recv.at[k], device_id=peer, device_id_type=MESH,
+            src_ref=source, dst_ref=target, send_sem=send_sem, recv_sem=recv_sem, device_id=peer, device_id_type=MESH,
         ))
         copies[-1].start()
-    value = part[pl.ds(a_at * chunk, chunk)]
-    for k in reversed(far_first(n)):
-        pltpu.make_async_copy(got_a.at[k], got_a.at[k], a_recv.at[k]).wait()
-        value = value + got_a[k]
-
-    def gather_sum(value, here, n, peers_, source, slots, send, recv):
+
+    def piece(half_of, at):
+        return pl.ds(half_of * count + at * chunk, chunk)
+
+    for (k, peer), (_, other) in zip(a_peers + [(0, None)], b_across):
+        if k:
+            own_piece = packed.at[piece(core, lax.rem(a_at + k, n))]
+            send(own_piece, got_a.at[0, k], a_send.at[0, k], a_recv.at[0, k], peer)
+        their_piece = packed.at[piece(1 - core, lax.rem(b_at + k, n))]
+        send(their_piece, got_a.at[1, k], a_send.at[1, k], a_recv.at[1, k], other)
+    value = packed[piece(core, a_at)]
+    for k in [0] + far_first(n)[::-1]:
+        for side in (0, 1) if k else (1,):
+            pltpu.make_async_copy(got_a.at[side, k], got_a.at[side, k], a_recv.at[side, k]).wait()
+            value = value + got_a[side, k]
+
+    def gather_sum(value, here, peers_, source, slots, send_sem, recv_sem):
         source[...] = value
         for k, peer in peers_:
-            copies.append(pltpu.make_async_remote_copy(
-                src_ref=source, dst_ref=slots.at[here], send_sem=send.at[k], recv_sem=recv.at[k],
-                device_id=peer, device_id_type=MESH,
-            ))
-            copies[-1].start()
+            send(source, slots.at[here], send_sem.at[k], recv_sem.at[k], peer)
         slots[pl.ds(here, 1)] = value[None]
-        for k in range(1, n):
-            pltpu.make_async_copy(source, source, recv.at[k]).wait()
+        for k in range(1, slots.shape[0]):
+            pltpu.make_async_copy(source, source, recv_sem.at[k]).wait()
         out = slots[0]
-        for i in range(1, n):
+        for i in range(1, slots.shape[0]):
             out = out + slots[i]
         return out
 
-    value = gather_sum(value, b_at, n, b_peers, sum_a, got_b, b_send, b_recv)
-    value = gather_sum(value, x, nx, x_peers, sum_b, got_x, x_send, x_recv)
-
-    def chunk_of(a_):
-        return fin.at[pl.ds(core * count + a_ * chunk, chunk)]
-
-    def pass_on(k, a_):
-        copies.append(pltpu.make_async_remote_copy(
-            src_ref=chunk_of(a_), dst_ref=chunk_of(a_), send_sem=f_send.at[k], recv_sem=f_recv.at[k],
-            device_id=mate, device_id_type=MESH,
-        ))
-        copies[-1].start()
-
-    fin[pl.ds(core * count + a_at * chunk, chunk)] = value
-    for k, peer in a_peers:
-        copies.append(pltpu.make_async_remote_copy(
-            src_ref=chunk_of(a_at), dst_ref=chunk_of(a_at), send_sem=g_send.at[k], recv_sem=g_recv.at[k],
-            device_id=peer, device_id_type=MESH,
-        ))
-        copies[-1].start()
-    pass_on(0, a_at)
-    for k in reversed(far_first(n)):
-        source = lax.rem(a_at + n - k, n)
-        pltpu.make_async_copy(chunk_of(source), chunk_of(source), g_recv.at[k]).wait()
-        pass_on(k, source)
+    value = gather_sum(value, b_at, b_peers, sum_a, got_b, b_send, b_recv)
+    value = gather_sum(value, x, x_peers, sum_b, got_x, x_send, x_recv)
+
+    mine = fin.at[piece(core, a_at)]
+    fin[piece(core, a_at)] = value
+    for (k, peer), (_, other) in zip(a_peers + [(0, None)], a_across):
+        if k:
+            send(mine, mine, g_send.at[0, k], g_recv.at[0, k], peer)
+        send(mine, mine, g_send.at[1, k], g_recv.at[1, k], other)
     for k in range(n):
-        source = lax.rem(b_at + n - k, n)
-        theirs = fin.at[pl.ds((1 - core) * count + source * chunk, chunk)]
-        pltpu.make_async_copy(theirs, theirs, f_recv.at[k]).wait()
+        if k:
+            same = fin.at[piece(core, lax.rem(a_at + n - k, n))]
+            pltpu.make_async_copy(same, same, g_recv.at[0, k]).wait()
+        theirs = fin.at[piece(1 - core, lax.rem(b_at + n - k, n))]
+        pltpu.make_async_copy(theirs, theirs, g_recv.at[1, k]).wait()
+
     for copy in copies:
         copy.wait_send()
 
@@ -296,12 +289,11 @@
         vmem((REACH, tile, k), BF16), vmem((REACH, tile, k), BF16),
         vmem((16, 128), F32), vmem((128, 16), F32), vmem(block, F32),
         vmem((k, 2 * k), F32),
-        vmem((2 * count, 8, 128), F32), vmem((count, 8, 128), F32), vmem((count, 8, 128), F32),
-        vmem((ny, chunk, 8, 128), F32), vmem((chunk, 8, 128), F32), vmem((nz, chunk, 8, 128), F32),
+        vmem((2 * count, 8, 128), F32),
+        vmem((2, ny, chunk, 8, 128), F32), vmem((chunk, 8, 128), F32), vmem((nz, chunk, 8, 128), F32),
         vmem((chunk, 8, 128), F32), vmem((nx, chunk, 8, 128), F32),
-        dma((4,)), dma((2 * REACH,)), dma((2 * REACH,)), dma((1,)), dma((1,)),
-        dma((ny,)), dma((ny,)), dma((nz,)), dma((nz,)), dma((nx,)), dma((nx,)),
-        dma((ny,)), dma((ny,)), dma((ny,)), dma((ny,)),
+        dma((4,)), dma((2 * REACH,)), dma((2 * REACH,)),
+        dma((2, ny)), dma((2, ny)), dma((nz,)), dma((nz,)), dma((nx,)), dma((nx,)), dma((2, ny)), dma((2, ny)),
     ]
     in_hbm = pl.BlockSpec(memory_space=pltpu.HBM)
     in_vmem = pl.BlockSpec(memory_space=pltpu.VMEM)
@@ -331,18 +323,20 @@
         lane = lax.broadcasted_iota(jnp.int32, (8, 128), 1)
         sub = lax.broadcasted_iota(jnp.int32, (8, 128), 0)
         groups = PANEL // 8
-        left = [work[8 * g : 8 * g + 8, 0:128] for g in range(groups)]
-        right = [work[8 * g : 8 * g + 8, 128:n] for g in range(groups)]
+        left = [work[0, 8 * g : 8 * g + 8] for g in range(groups)]
+        right = [work[1, 8 * g : 8 * g + 8] for g in range(groups)]
         for m in range(PANEL // PIVOT):
             c0 = m * PIVOT
             g0, s0 = c0 // 8, c0 % 8
             inside = (lane >= c0) & (lane < c0 + PIVOT)
-            cols = [[jnp.broadcast_to(left[g][:, c0 + q : c0 + q + 1], (8, 128)) for q in range(PIVOT)]
-                    for g in range(g0, groups)]
-            pick = lambda r, q: jnp.broadcast_to(cols[0][q][s0 + r : s0 + r + 1, :], (8, 128))
-            piv = {(r, q): pick(r, q) for q in range(PIVOT) for r in range(q, PIVOT)}
-            row_l = [jnp.broadcast_to(left[g0][s0 + q : s0 + q + 1, :], (8, 128)) for q in range(PIVOT)]
-            row_r = [jnp.broadcast_to(right[g0][s0 + q : s0 + q + 1, :], (8, 128)) for q in range(PIVOT)]
+            row_l = [work[0, pl.ds(c0 + q, 8, stride=0), :] for q in range(PIVOT)]
+            row_r = [work[1, pl.ds(c0 + q, 8, stride=0), :] for q in range(PIVOT)]
+
+            def lane_of(v, at):
+                return jnp.broadcast_to(v[:, at : at + 1], (8, 128))
+
+            piv = {(r, q): lane_of(row_l[q], c0 + r) for q in range(PIVOT) for r in range(q, PIVOT)}
+            cols = [[lane_of(left[g], c0 + q) for q in range(PIVOT)] for g in range(g0, groups)]
             row_l = [jnp.where(inside, jnp.where(lane == c0 + q, 1.0, 0.0), row_l[q]) for q in range(PIVOT)]
             u = {}
             inv = []
@@ -387,6 +381,9 @@
                     cleared = cleared - w[q] * z_l[q]
                     right[g] = right[g] - w[q] * z_r[q]
                 left[g] = cleared
+                if g == (c0 + PIVOT) // 8:
+                    work[0, 8 * g : 8 * g + 8] = left[g]
+                    work[1, 8 * g : 8 * g + 8] = right[g]
 
         at = lax.broadcasted_iota(jnp.int32, (PANEL, n), 1)
         below_diagonal = at <= lax.broadcasted_iota(jnp.int32, (PANEL, n), 0)
@@ -395,24 +392,26 @@
         rhs = jnp.concatenate([b1, b2, b1, b2, b3, b1], axis=0)
         update = lax.dot_general(lhs, rhs, (((0,), (0,)), ((), ())), preferred_element_type=F32)
         lanes = lax.broadcasted_iota(jnp.int32, (n - PANEL, n), 1)
-        fresh = jnp.where(lanes < PANEL, 0.0, work[PANEL:, :]) - update[PANEL:, :]
-        work[0 : n - PANEL, :] = pltpu.roll(fresh, n - PANEL, 1)
+        old = jnp.concatenate([work[0, PANEL:], work[1, PANEL:]], axis=1)
+        fresh = pltpu.roll(jnp.where(lanes < PANEL, 0.0, old) - update[PANEL:, :], n - PANEL, 1)
+        work[0, 0 : n - PANEL] = fresh[:, 0:128]
+        work[1, 0 : n - PANEL] = fresh[:, 128:]
         return carry
 
     lax.fori_loop(0, n // PANEL, panel, 0)
 
 
-def back_kernel(cols_hbm, gram_ref, high_v, low_v, basis_hbm, factor_ref,
-                cols_ref, out_v, work, rows_w, rows_f, w_high, w_low, load_sem, out_sem):
-    n = work.shape[0]
+def back_kernel(cols_hbm, gram_ref, high_v, low_v, basis_hbm, factor_hbm,
+                cols_ref, factor_ref, out_v, work, rows_w, rows_f, w_high, w_low, load_sem, out_sem):
+    n = work.shape[1]
     half = n // 2
     load_cols = pltpu.make_async_copy(cols_hbm, cols_ref, load_sem.at[0])
     load_cols.start()
     upper = gram_ref[16:32].reshape(half, half)
-    work[0:half, 0:half] = gram_ref[0:16].reshape(half, half)
-    work[0:half, half:] = upper
-    work[half:, 0:half] = upper.T
-    work[half:, half:] = gram_ref[32:48].reshape(half, half)
+    work[0, 0:half] = gram_ref[0:16].reshape(half, half)
+    work[1, 0:half] = upper
+    work[0, half:] = upper.T
+    work[1, half:] = gram_ref[32:48].reshape(half, half)
     factor_in_place(work, rows_w, rows_f, n)
 
     for p in range(n // PANEL):
@@ -429,9 +428,10 @@
         w_low[rows, :] = (w - high.astype(F32)).astype(BF16)
 
     load_cols.wait()
+    writes = [pltpu.make_async_copy(factor_ref, factor_hbm, out_sem.at[LINES])]
+    writes[0].start()
     wh, wl = w_high[...], w_low[...]
     weights = jnp.concatenate([wh, wl, wh], axis=1)
-    writes = []
     for t in range(LINES):
         head = t // REACH * REACH
         start = cols_ref[head, REACH]
@@ -459,11 +459,11 @@
         back_kernel,
         out_shape=(jax.ShapeDtypeStruct((lines, tile, k), F32), jax.ShapeDtypeStruct((k, k), F32)),
         in_specs=[in_hbm, in_vmem, in_vmem, in_vmem],
-        out_specs=(in_hbm, in_vmem),
+        out_specs=(in_hbm, in_hbm),
         scratch_shapes=[
-            pltpu.SMEM(tile_cols.shape, jnp.int32), vmem((lines, tile, k), F32),
-            vmem((k, k), F32), vmem((k // PANEL, PANEL, k), F32), vmem((k // PANEL, PANEL, k), F32),
-            vmem((k, k), BF16), vmem((k, k), BF16), dma((1,)), dma((lines,)),
+            pltpu.SMEM(tile_cols.shape, jnp.int32), vmem((k, k), F32), vmem((lines, tile, k), F32),
+            vmem((2, k, k // 2), F32), vmem((k // PANEL, PANEL, k), F32), vmem((k // PANEL, PANEL, k), F32),
+            vmem((k, k), BF16), vmem((k, k), BF16), dma((1,)), dma((lines + 1,)),
         ],
         compiler_params=pltpu.CompilerParams(vmem_limit_bytes=48 * 2**20),
         name="back",

time: 63.9 us -> 61.5 us (0.962)
  Pallas kernels: 63.1 us -> 60.7 us
    pallas_call x1, Pallas kernels: 12 us -> 10 us  [back(): pl.pallas_call(back_kernel, out_shape=(jax.ShapeDtypeStruct((lines, tile,...]
where the time goes in v3:
time: 61.5 us; the launch traced here: 61.4 us
  Pallas kernels  60.7 us (99%)
  between operations  0.64 us (1%)
    pallas_call x1, Pallas kernels, front(): pl.pallas_call(functools.partial(front_kernel, sizes, 1.0 / total), out_s...  50.7 us
    pallas_call x1, Pallas kernels, back(): pl.pallas_call(back_kernel, out_shape=(jax.ShapeDtypeStruct((lines, tile,...  10 us

profile of v3, /device:TPU:1, one launch (start us, length us, event | category | flops | bytes accessed | tf_op | source)
XLA Modules:
  0.0 61.4 jit_solution(13733119038971536648)
XLA Ops:
  0.6 50.7 %front.1 = (bf16[8,256,256]{2,1,0:T(8,128)(2,1)S(1)}, bf16[8,256,256]{2,1,0:T(8,128)(2,1)S(1)}, f32[48,8,128]{2,1,0:T(8,128)S(1)}) custom-call(s32[8,9]{1,0:T(8,128)} %cols_hbm.3, f32[8,2,128]{2,1,0:T(2,128)} %bitcast.4, bf16[8,256,256]{2,1,0:T(8,128)(2,1)} %bitcast.3, bf16[9,256,256]{2,1,0:T(8,128)(2,1)} %cov_hbm.1), custom_call_target="tpu_custom_call" | custom-call | tf_op jit(solution)/shard_map/front/pallas_call | solution.py:300
  51.3 10.0 %back.1 = (f32[8,256,256]{2,1,0:T(8,128)}, f32[256,256]{1,0:T(8,128)}) custom-call(s32[8,9]{1,0:T(8,128)} %cols_hbm.3, f32[48,8,128]{2,1,0:T(8,128)S(1)} %get-tuple-element.7.gram_ref, bf16[8,256,256]{2,1,0:T(8,128)(2,1)S(1)} %get-tuple-element.8.high_v, bf16[8,256,256]{2,1,0:T(8,128)(2,1)S(1)} %get-tuple-element.9.low_v), custom_call_target="tpu_custom_call" | custom-call | tf_op jit(solution)/shard_map/back/pallas_call | solution.py:458

commit v4 on v3

--- a/solution.py
+++ b/solution.py
@@ -28,10 +28,9 @@
 
 def front_kernel(
     sizes, scale, cols_hbm, std_hbm, sketch_hbm, cov_hbm, high_v, low_v, fin,
-    cols_ref, std_ref, sketch_v, cov_v, own, below, above, std_sorted, std_cols, acc, gacc,
+    cols_ref, std_ref, sketch_v, cov_v, own, near, far, std_sorted, std_rows, acc, gacc,
     packed, got_a, sum_a, got_b, sum_b, got_x,
-    load_sem, halo_send, halo_recv, a_send, a_recv,
-    b_send, b_recv, x_send, x_recv, g_send, g_recv,
+    load_sem, halo_send, halo_recv, send_sem, recv_sem,
 ):
     nx, ny, nzh, nzl = sizes["nx"], sizes["ny"], sizes["nzh"], sizes["nzl"]
     nz = nzh * nzl
@@ -52,7 +51,6 @@
 
     outer = jnp.where(core == 0, me - 1, me + 1)
     has_outer = (outer >= 0) & (outer < total)
-    has_low, has_high = me > 0, me < total - 1
 
     load_cols = pltpu.make_async_copy(cols_hbm, cols_ref, load_sem.at[0])
     load_std = pltpu.make_async_copy(std_hbm, std_ref, load_sem.at[1])
@@ -83,13 +81,9 @@
     own[0:REACH] = zero_lines
     own[REACH + LINES :] = zero_lines
 
-    @pl.when(jnp.logical_not(has_low))
+    @pl.when(jnp.logical_not(has_outer))
     def _():
-        below[...] = zero_lines
-
-    @pl.when(jnp.logical_not(has_high))
-    def _():
-        above[...] = zero_lines
+        far[...] = zero_lines
 
     load_cols.wait()
     tile_of_line = []
@@ -106,14 +100,16 @@
     load_std.wait()
     for j in range(LINES):
         std_sorted[2 * j : 2 * j + 2, :] = std_ref[tile_of_line[j]]
-    std_cols[...] = std_sorted[...].T
-
-    def std_of(j):
-        return jnp.concatenate([std_cols[:, 2 * j : 2 * j + 1], std_cols[:, 2 * j + 1 : 2 * j + 2]], axis=0)
+    std_cols = std_sorted[...].T
+
+    def times_std(value, j):
+        return value * jnp.concatenate([std_rows[j], std_rows[j]], axis=1)
 
     def scale_lines(q):
         for j in (q, LINES - 1 - q):
-            own[REACH + j] = (sketch_v[tile_of_line[j]].astype(F32) * std_of(j)).astype(BF16)
+            both = [jnp.broadcast_to(std_cols[:, c : c + 1], (128, 128)) for c in (2 * j, 2 * j + 1)]
+            std_rows[j] = jnp.concatenate(both, axis=0)
+            own[REACH + j] = times_std(sketch_v[tile_of_line[j]].astype(F32), j).astype(BF16)
 
     load_sketch.wait()
     scale_lines(0)
@@ -133,27 +129,25 @@
     peers = len(z_peers + y_peers + x_peers + y_across + z_across) - 1
     pl.semaphore_wait(barrier, peers + jnp.where(has_outer, 1, 0))
 
-    def to_low(q):
+    def to_near(q):
         return pltpu.make_async_remote_copy(
-            src_ref=own.at[REACH + q], dst_ref=above.at[q], send_sem=halo_send.at[q],
-            recv_sem=halo_recv.at[q], device_id=linear(me - 1), device_id_type=MESH,
+            src_ref=own.at[REACH + jnp.where(core == 0, LINES - 1 - q, q)], dst_ref=near.at[q], send_sem=halo_send.at[q],
+            recv_sem=halo_recv.at[q], device_id=place(x, y, z, 1 - core), device_id_type=MESH,
         )
 
-    def to_high(q):
+    def to_far(q):
         return pltpu.make_async_remote_copy(
-            src_ref=own.at[REACH + LINES - 1 - q], dst_ref=below.at[q], send_sem=halo_send.at[REACH + q],
-            recv_sem=halo_recv.at[REACH + q], device_id=linear(me + 1), device_id_type=MESH,
+            src_ref=own.at[REACH + jnp.where(core == 0, q, LINES - 1 - q)], dst_ref=far.at[q],
+            send_sem=halo_send.at[REACH + q], recv_sem=halo_recv.at[REACH + q], device_id=linear(outer),
+            device_id_type=MESH,
         )
 
     for q in range(REACH):
-        @pl.when(has_low)
+        @pl.when(has_outer)
         def _():
-            to_low(q).start()
-
-        @pl.when(has_high)
-        def _():
-            to_high(q).start()
-
+            to_far(q).start()
+
+        to_near(q).start()
         if q + 2 < REACH:
             scale_lines(q + 2)
 
@@ -168,7 +162,7 @@
     lax.fori_loop(0, LINES, own_line, 0)
 
     def finish(j, product):
-        latent = product * std_of(j)
+        latent = times_std(product, j)
         high = latent.astype(BF16)
         low = (latent - high.astype(F32)).astype(BF16)
         high_v[j] = high
@@ -176,30 +170,25 @@
         pair = jnp.concatenate([high, low], axis=1)
         gacc[...] += lax.dot_general(high, pair, (((0,), (0,)), ((), ())), preferred_element_type=F32)
 
+    def add_line(line, q, upper):
+        for t in range(REACH - q):
+            j = jnp.where(upper, REACH + q + t, REACH - 1 - q - t)
+            e = jnp.where(upper, LAGS - 1 - t, t)
+            product = acc[j] + jnp.dot(cov_v[e], line, preferred_element_type=F32)
+            if t:
+                acc[j] = product
+            else:
+                finish(j, product)
+
     for q in range(REACH):
-        @pl.when(has_low)
+        to_near(q).wait_recv()
+        add_line(near[q], q, core == 0)
+    for q in range(REACH):
+        @pl.when(has_outer)
         def _():
-            to_high(q).wait_recv()
-
-        for j in range(REACH - q):
-            e = (-1 - q) - j + REACH
-            product = acc[j] + jnp.dot(cov_v[e], below[q], preferred_element_type=F32)
-            if j == REACH - 1 - q:
-                finish(j, product)
-            else:
-                acc[j] = product
-
-        @pl.when(has_high)
-        def _():
-            to_low(q).wait_recv()
-
-        for j in range(REACH + q, LINES):
-            e = (LINES + q) - j + REACH
-            product = acc[j] + jnp.dot(cov_v[e], above[q], preferred_element_type=F32)
-            if j == REACH + q:
-                finish(j, product)
-            else:
-                acc[j] = product
+            to_far(q).wait_recv()
+
+        add_line(far[q], q, core == 1)
 
     half = gacc.shape[0] // 2
     for block, (r, c) in enumerate(((0, 0), (0, half), (half, half))):
@@ -210,13 +199,16 @@
 
     count = packed.shape[0] // 2
     chunk = count // n
-    copies = []
-
-    def send(source, target, send_sem, recv_sem, peer):
-        copies.append(pltpu.make_async_remote_copy(
-            src_ref=source, dst_ref=target, send_sem=send_sem, recv_sem=recv_sem, device_id=peer, device_id_type=MESH,
-        ))
-        copies[-1].start()
+
+    def send(source, target, step, peer):
+        pltpu.make_async_remote_copy(
+            src_ref=source, dst_ref=target, send_sem=send_sem.at[step], recv_sem=recv_sem.at[step], device_id=peer,
+            device_id_type=MESH,
+        ).start()
+
+    def wait(sem, chunks):
+        bytes_of = packed.at[pl.ds(0, chunks * chunk)]
+        pltpu.make_async_copy(bytes_of, bytes_of, sem).wait()
 
     def piece(half_of, at):
         return pl.ds(half_of * count + at * chunk, chunk)
@@ -224,55 +216,46 @@
     for (k, peer), (_, other) in zip(a_peers + [(0, None)], b_across):
         if k:
             own_piece = packed.at[piece(core, lax.rem(a_at + k, n))]
-            send(own_piece, got_a.at[0, k], a_send.at[0, k], a_recv.at[0, k], peer)
+            send(own_piece, got_a.at[0, k], 0, peer)
         their_piece = packed.at[piece(1 - core, lax.rem(b_at + k, n))]
-        send(their_piece, got_a.at[1, k], a_send.at[1, k], a_recv.at[1, k], other)
+        send(their_piece, got_a.at[1, k], 0, other)
     value = packed[piece(core, a_at)]
-    for k in [0] + far_first(n)[::-1]:
+    wait(recv_sem.at[0], 2 * n - 1)
+    for k in range(n):
         for side in (0, 1) if k else (1,):
-            pltpu.make_async_copy(got_a.at[side, k], got_a.at[side, k], a_recv.at[side, k]).wait()
             value = value + got_a[side, k]
 
-    def gather_sum(value, here, peers_, source, slots, send_sem, recv_sem):
+    def gather_sum(value, here, peers_, source, slots, step):
         source[...] = value
-        for k, peer in peers_:
-            send(source, slots.at[here], send_sem.at[k], recv_sem.at[k], peer)
+        for _, peer in peers_:
+            send(source, slots.at[here], step, peer)
         slots[pl.ds(here, 1)] = value[None]
-        for k in range(1, slots.shape[0]):
-            pltpu.make_async_copy(source, source, recv_sem.at[k]).wait()
+        wait(recv_sem.at[step], slots.shape[0] - 1)
         out = slots[0]
         for i in range(1, slots.shape[0]):
             out = out + slots[i]
         return out
 
-    value = gather_sum(value, b_at, b_peers, sum_a, got_b, b_send, b_recv)
-    value = gather_sum(value, x, x_peers, sum_b, got_x, x_send, x_recv)
+    value = gather_sum(value, b_at, b_peers, sum_a, got_b, 1)
+    value = gather_sum(value, x, x_peers, sum_b, got_x, 2)
 
     mine = fin.at[piece(core, a_at)]
     fin[piece(core, a_at)] = value
     for (k, peer), (_, other) in zip(a_peers + [(0, None)], a_across):
         if k:
-            send(mine, mine, g_send.at[0, k], g_recv.at[0, k], peer)
-        send(mine, mine, g_send.at[1, k], g_recv.at[1, k], other)
-    for k in range(n):
-        if k:
-            same = fin.at[piece(core, lax.rem(a_at + n - k, n))]
-            pltpu.make_async_copy(same, same, g_recv.at[0, k]).wait()
-        theirs = fin.at[piece(1 - core, lax.rem(b_at + n - k, n))]
-        pltpu.make_async_copy(theirs, theirs, g_recv.at[1, k]).wait()
-
-    for copy in copies:
-        copy.wait_send()
-
-    @pl.when(has_low)
+            send(mine, mine, 3, peer)
+        send(mine, mine, 3, other)
+    wait(recv_sem.at[3], 2 * n - 1)
+    for step, chunks in enumerate((2 * n - 1, n - 1, nx - 1, 2 * n - 1)):
+        wait(send_sem.at[step], chunks)
+
+    for q in range(REACH):
+        to_near(q).wait_send()
+
+    @pl.when(has_outer)
     def _():
         for q in range(REACH):
-            to_low(q).wait_send()
-
-    @pl.when(has_high)
-    def _():
-        for q in range(REACH):
-            to_high(q).wait_send()
+            to_far(q).wait_send()
 
 
 def front(sizes, sketch, marginal_std, cov_tiles, tile_cols):
@@ -287,13 +270,13 @@
     scratch = [
         pltpu.SMEM(tile_cols.shape, jnp.int32), vmem((LINES, 2, 128), F32), vmem(block, BF16), vmem(cov_tiles.shape, BF16), vmem((2 * REACH + LINES, tile, k), BF16),
         vmem((REACH, tile, k), BF16), vmem((REACH, tile, k), BF16),
-        vmem((16, 128), F32), vmem((128, 16), F32), vmem(block, F32),
+        vmem((16, 128), F32), vmem((LINES, tile, 128), F32), vmem(block, F32),
         vmem((k, 2 * k), F32),
         vmem((2 * count, 8, 128), F32),
         vmem((2, ny, chunk, 8, 128), F32), vmem((chunk, 8, 128), F32), vmem((nz, chunk, 8, 128), F32),
         vmem((chunk, 8, 128), F32), vmem((nx, chunk, 8, 128), F32),
         dma((4,)), dma((2 * REACH,)), dma((2 * REACH,)),
-        dma((2, ny)), dma((2, ny)), dma((nz,)), dma((nz,)), dma((nx,)), dma((nx,)), dma((2, ny)), dma((2, ny)),
+        dma((4,)), dma((4,)),
     ]
     in_hbm = pl.BlockSpec(memory_space=pltpu.HBM)
     in_vmem = pl.BlockSpec(memory_space=pltpu.VMEM)
@@ -318,8 +301,23 @@
     return a1, a2, (rest - a2.astype(F32)).astype(BF16)
 
 
-def factor_in_place(work, rows_w, rows_f, n):
+def stacked(b):
+    b1, b2, b3 = split3(b)
+    return jnp.concatenate([b1, b1, b2, b2, b1, b3], axis=0), jnp.concatenate([b1, b2, b1, b2, b3, b1], axis=0)
+
+
+def factor_in_place(work, rest, late, rows_w, rows_f, n):
     def panel(p, carry):
+        lanes = lax.broadcasted_iota(jnp.int32, (n - PANEL, n), 1)
+        lhs, rhs = stacked(late[...])
+        update = lax.dot_general(lhs, rhs, (((0,), (0,)), ((), ())), preferred_element_type=F32)
+        old = jnp.concatenate([rest[0], rest[1]], axis=1)
+        fresh = jnp.where(lanes >= jnp.where(p > 0, n - PANEL, n), 0.0, old) - update[PANEL:]
+        following = pltpu.roll(jnp.where(lanes[:PANEL] < PANEL, 0.0, fresh[:PANEL]), n - PANEL, 1)
+        fresh = pltpu.roll(fresh[PANEL:], n - PANEL, 1)
+        rest[0, 0 : n - 2 * PANEL] = fresh[:, 0:128]
+        rest[1, 0 : n - 2 * PANEL] = fresh[:, 128:]
+
         lane = lax.broadcasted_iota(jnp.int32, (8, 128), 1)
         sub = lax.broadcasted_iota(jnp.int32, (8, 128), 0)
         groups = PANEL // 8
@@ -387,32 +385,34 @@
 
         at = lax.broadcasted_iota(jnp.int32, (PANEL, n), 1)
         below_diagonal = at <= lax.broadcasted_iota(jnp.int32, (PANEL, n), 0)
-        b1, b2, b3 = split3(jnp.where(below_diagonal | (at >= PANEL), rows_w[p], 0.0))
-        lhs = jnp.concatenate([b1, b1, b2, b2, b1, b3], axis=0)
-        rhs = jnp.concatenate([b1, b2, b1, b2, b3, b1], axis=0)
-        update = lax.dot_general(lhs, rhs, (((0,), (0,)), ((), ())), preferred_element_type=F32)
-        lanes = lax.broadcasted_iota(jnp.int32, (n - PANEL, n), 1)
-        old = jnp.concatenate([work[0, PANEL:], work[1, PANEL:]], axis=1)
-        fresh = pltpu.roll(jnp.where(lanes < PANEL, 0.0, old) - update[PANEL:, :], n - PANEL, 1)
-        work[0, 0 : n - PANEL] = fresh[:, 0:128]
-        work[1, 0 : n - PANEL] = fresh[:, 128:]
+        rows = jnp.where(below_diagonal | (at >= PANEL), rows_w[p], 0.0)
+        lhs, rhs = stacked(rows)
+        update = lax.dot_general(lhs[:, 0:128], rhs, (((0,), (0,)), ((), ())), preferred_element_type=F32)
+        following = following - pltpu.roll(update[PANEL : 2 * PANEL], n - PANEL, 1)
+        work[0] = following[:, 0:128]
+        work[1] = following[:, 128:]
+        late[...] = pltpu.roll(rows, n - PANEL, 1)
         return carry
 
+    late[...] = jnp.zeros_like(late)
     lax.fori_loop(0, n // PANEL, panel, 0)
 
 
 def back_kernel(cols_hbm, gram_ref, high_v, low_v, basis_hbm, factor_hbm,
-                cols_ref, factor_ref, out_v, work, rows_w, rows_f, w_high, w_low, load_sem, out_sem):
-    n = work.shape[1]
+                cols_ref, factor_ref, out_v, work, rest, late, rows_w, rows_f, w_high, w_low, load_sem, out_sem):
+    n = factor_ref.shape[0]
     half = n // 2
     load_cols = pltpu.make_async_copy(cols_hbm, cols_ref, load_sem.at[0])
     load_cols.start()
     upper = gram_ref[16:32].reshape(half, half)
-    work[0, 0:half] = gram_ref[0:16].reshape(half, half)
-    work[1, 0:half] = upper
-    work[0, half:] = upper.T
-    work[1, half:] = gram_ref[32:48].reshape(half, half)
-    factor_in_place(work, rows_w, rows_f, n)
+    first = gram_ref[0:16].reshape(half, half)
+    work[0] = first[:PANEL]
+    work[1] = upper[:PANEL]
+    rest[0, 0 : half - PANEL] = first[PANEL:]
+    rest[1, 0 : half - PANEL] = upper[PANEL:]
+    rest[0, half - PANEL :] = upper.T
+    rest[1, half - PANEL :] = gram_ref[32:48].reshape(half, half)
+    factor_in_place(work, rest, late, rows_w, rows_f, n)
 
     for p in range(n // PANEL):
         rows = slice(p * PANEL, p * PANEL + PANEL)
@@ -462,7 +462,8 @@
         out_specs=(in_hbm, in_hbm),
         scratch_shapes=[
             pltpu.SMEM(tile_cols.shape, jnp.int32), vmem((k, k), F32), vmem((lines, tile, k), F32),
-            vmem((2, k, k // 2), F32), vmem((k // PANEL, PANEL, k), F32), vmem((k // PANEL, PANEL, k), F32),
+            vmem((2, PANEL, k // 2), F32), vmem((2, k - PANEL, k // 2), F32), vmem((PANEL, k), F32),
+            vmem((k // PANEL, PANEL, k), F32), vmem((k // PANEL, PANEL, k), F32),
             vmem((k, k), BF16), vmem((k, k), BF16), dma((1,)), dma((lines + 1,)),
         ],
         compiler_params=pltpu.CompilerParams(vmem_limit_bytes=48 * 2**20),

time: 61.5 us -> 60 us (0.976)
  Pallas kernels: 60.7 us -> 59.2 us
    pallas_call x1, Pallas kernels: 50.7 us -> 49.5 us  [front(): pl.pallas_call(functools.partial(front_kernel, sizes, 1.0 / total), out_s...]
where the time goes in v4:
time: 60 us; the launch traced here: 59.8 us
  Pallas kernels  59.2 us (99%)
  between operations  0.64 us (1%)
    pallas_call x1, Pallas kernels, front(): pl.pallas_call(functools.partial(front_kernel, sizes, 1.0 / total), out_s...  49.5 us
    pallas_call x1, Pallas kernels, back(): pl.pallas_call(back_kernel, out_shape=(jax.ShapeDtypeStruct((lines, tile,...  9.71 us

profile of v4, /device:TPU:1, one launch (start us, length us, event | category | flops | bytes accessed | tf_op | source)
XLA Modules:
  0.0 59.8 jit_solution(5647595048411504777)
XLA Ops:
  0.6 49.5 %front.1 = (bf16[8,256,256]{2,1,0:T(8,128)(2,1)S(1)}, bf16[8,256,256]{2,1,0:T(8,128)(2,1)S(1)}, f32[48,8,128]{2,1,0:T(8,128)S(1)}) custom-call(s32[8,9]{1,0:T(8,128)} %cols_hbm.3, f32[8,2,128]{2,1,0:T(2,128)} %bitcast.4, bf16[8,256,256]{2,1,0:T(8,128)(2,1)} %bitcast.3, bf16[9,256,256]{2,1,0:T(8,128)(2,1)} %cov_hbm.1), custom_call_target="tpu_custom_call" | custom-call | tf_op jit(solution)/shard_map/front/pallas_call | solution.py:283
  50.1 9.7 %back.1 = (f32[8,256,256]{2,1,0:T(8,128)}, f32[256,256]{1,0:T(8,128)}) custom-call(s32[8,9]{1,0:T(8,128)} %cols_hbm.3, f32[48,8,128]{2,1,0:T(8,128)S(1)} %get-tuple-element.7.gram_ref, bf16[8,256,256]{2,1,0:T(8,128)(2,1)S(1)} %get-tuple-element.8.high_v, bf16[8,256,256]{2,1,0:T(8,128)(2,1)S(1)} %get-tuple-element.9.low_v), custom_call_target="tpu_custom_call" | custom-call | tf_op jit(solution)/shard_map/back/pallas_call | solution.py:458

commit v5 on v4

--- a/solution.py
+++ b/solution.py
@@ -56,7 +56,7 @@
     load_std = pltpu.make_async_copy(std_hbm, std_ref, load_sem.at[1])
     load_sketch = pltpu.make_async_copy(sketch_hbm, sketch_v, load_sem.at[2])
     load_cov = pltpu.make_async_copy(cov_hbm, cov_v, load_sem.at[3])
-    for copy in (load_cols, load_std, load_sketch, load_cov):
+    for copy in (load_cols, load_std, load_sketch):
         copy.start()
 
     barrier = pltpu.get_barrier_semaphore()
@@ -112,6 +112,7 @@
             own[REACH + j] = times_std(sketch_v[tile_of_line[j]].astype(F32), j).astype(BF16)
 
     load_sketch.wait()
+    load_cov.start()
     scale_lines(0)
     scale_lines(1)
 
@@ -131,14 +132,14 @@
 
     def to_near(q):
         return pltpu.make_async_remote_copy(
-            src_ref=own.at[REACH + jnp.where(core == 0, LINES - 1 - q, q)], dst_ref=near.at[q], send_sem=halo_send.at[q],
+            src_ref=own.at[REACH + jnp.where(core == 0, LINES - 1 - q, q)], dst_ref=near.at[q], send_sem=halo_send.at[0],
             recv_sem=halo_recv.at[q], device_id=place(x, y, z, 1 - core), device_id_type=MESH,
         )
 
     def to_far(q):
         return pltpu.make_async_remote_copy(
             src_ref=own.at[REACH + jnp.where(core == 0, q, LINES - 1 - q)], dst_ref=far.at[q],
-            send_sem=halo_send.at[REACH + q], recv_sem=halo_recv.at[REACH + q], device_id=linear(outer),
+            send_sem=halo_send.at[1], recv_sem=halo_recv.at[REACH + q], device_id=linear(outer),
             device_id_type=MESH,
         )
 
@@ -249,13 +250,11 @@
     for step, chunks in enumerate((2 * n - 1, n - 1, nx - 1, 2 * n - 1)):
         wait(send_sem.at[step], chunks)
 
-    for q in range(REACH):
-        to_near(q).wait_send()
+    pltpu.make_async_copy(near, near, halo_send.at[0]).wait()
 
     @pl.when(has_outer)
     def _():
-        for q in range(REACH):
-            to_far(q).wait_send()
+        pltpu.make_async_copy(far, far, halo_send.at[1]).wait()
 
 
 def front(sizes, sketch, marginal_std, cov_tiles, tile_cols):
@@ -275,7 +274,7 @@
         vmem((2 * count, 8, 128), F32),
         vmem((2, ny, chunk, 8, 128), F32), vmem((chunk, 8, 128), F32), vmem((nz, chunk, 8, 128), F32),
         vmem((chunk, 8, 128), F32), vmem((nx, chunk, 8, 128), F32),
-        dma((4,)), dma((2 * REACH,)), dma((2 * REACH,)),
+        dma((4,)), dma((2,)), dma((2 * REACH,)),
         dma((4,)), dma((4,)),
     ]
     in_hbm = pl.BlockSpec(memory_space=pltpu.HBM)

time: 60 us -> 59.9 us (level)
  no operation moved by 1% of the time
where the time goes in v5:
time: 59.9 us; the launch traced here: 59.8 us
  Pallas kernels  59.1 us (99%)
  between operations  0.64 us (1%)
    pallas_call x1, Pallas kernels, front(): pl.pallas_call(functools.partial(front_kernel, sizes, 1.0 / total), out_s...  49.4 us
    pallas_call x1, Pallas kernels, back(): pl.pallas_call(back_kernel, out_shape=(jax.ShapeDtypeStruct((lines, tile,...  9.71 us

profile of v5, /device:TPU:1, one launch (start us, length us, event | category | flops | bytes accessed | tf_op | source)
XLA Modules:
  0.0 59.8 jit_solution(12443230310700452892)
XLA Ops:
  0.6 49.4 %front.1 = (bf16[8,256,256]{2,1,0:T(8,128)(2,1)S(1)}, bf16[8,256,256]{2,1,0:T(8,128)(2,1)S(1)}, f32[48,8,128]{2,1,0:T(8,128)S(1)}) custom-call(s32[8,9]{1,0:T(8,128)} %cols_hbm.3, f32[8,2,128]{2,1,0:T(2,128)} %bitcast.4, bf16[8,256,256]{2,1,0:T(8,128)(2,1)} %bitcast.3, bf16[9,256,256]{2,1,0:T(8,128)(2,1)} %cov_hbm.1), custom_call_target="tpu_custom_call" | custom-call | tf_op jit(solution)/shard_map/front/pallas_call | solution.py:282
  50.1 9.7 %back.1 = (f32[8,256,256]{2,1,0:T(8,128)}, f32[256,256]{1,0:T(8,128)}) custom-call(s32[8,9]{1,0:T(8,128)} %cols_hbm.3, f32[48,8,128]{2,1,0:T(8,128)S(1)} %get-tuple-element.7.gram_ref, bf16[8,256,256]{2,1,0:T(8,128)(2,1)S(1)} %get-tuple-element.8.high_v, bf16[8,256,256]{2,1,0:T(8,128)(2,1)S(1)} %get-tuple-element.9.low_v), custom_call_target="tpu_custom_call" | custom-call | tf_op jit(solution)/shard_map/back/pallas_call | solution.py:457
